TPU v7x, 128 devices: a whole 4x4x4 slice. The times are simulated.
128 devices in a mesh: seq: 16 (over z, x), tensor: 8 (over y, core).
Axes of the slice: x: 4, y: 4, z: 4, core: 2. Of those that a mesh axis runs over, the one named last changes fastest.
Arguments:
- queries: bfloat16 [16384, 8192], P('seq', 'tensor'), may hold values from -6 to 6
- keys: bfloat16 [16384, 1024], P('seq', 'tensor'), may hold values from -6 to 6
- values: bfloat16 [16384, 1024], P('seq', 'tensor'), may hold values from -6 to 6
- key_blocks: int32 [64, 128, 16], P('tensor'), may hold values from 0 to 127, as said below
- block_counts: int32 [64, 128], P('tensor'), may hold values from 1 to 16, as said below
- out_weight: bfloat16 [8192, 8192], P('tensor'), may hold values from -0.59765625 to 0.59765625
Outputs:
- projected: bfloat16 [16384, 8192], P('seq', 'tensor')
Inputs may be any that keep to these rules, and one draw needn't show every extreme that they name: For head h and query block b the first block_counts[h, b] entries of key_blocks[h, b] are different blocks of 0 to b, the first being b itself; the later entries are block numbers without meaning. block_counts[h, b] is at most b + 1; the last query block of every head has exactly 16.
All inputs are finite; a program needn't handle non-finite values.
Results may differ from a plain program's by a relative error of at most 0.014.
Values may be sent and summed in bfloat16 or wider, within the bound.
No kernel may reach another device: no remote copies, remote signals or barrier semaphores. Data moves between devices by JAX's collectives and lax.ppermute only.
A program may use at most 128 MiB of HBM per device.

v0:
```python
import functools
import math

import jax
import jax.numpy as jnp
from jax import lax
from jax.experimental import pallas as pl
from jax.experimental.pallas import tpu as pltpu
from jax.sharding import PartitionSpec as P

HEAD_DIM = 128
BLOCK = 128
SIDE = 4
CORES = 2
PARTS = 8
CHUNKS = (3, 3, 2)
VARIANTS = (1, 2, 3, 4, 6, 8)
ORDER = (2, 1, 3, 0)
COST = 2
NEG = -1e30


def along_x(step):
    return [(z * SIDE + x, z * SIDE + (x + step) % SIDE) for z in range(SIDE) for x in range(SIDE)]


def along_z(step):
    return [(z * SIDE + x, (z + step) % SIDE * SIDE + x) for z in range(SIDE) for x in range(SIDE)]


def along_y(step):
    return [(y * CORES + c, (y + step) % SIDE * CORES + c) for y in range(SIDE) for c in range(CORES)]


def other_core():
    return [(y * CORES + c, y * CORES + CORES - 1 - c) for y in range(SIDE) for c in range(CORES)]


def ring(piece, perm):
    half = piece.shape[0] // 2
    before = lax.ppermute(piece, "seq", perm(1))
    after = lax.ppermute(piece, "seq", perm(-1))
    far_low = lax.ppermute(before[:half], "seq", perm(1))
    far_high = lax.ppermute(after[half:], "seq", perm(-1))
    return before, after, far_low, far_high


def gather(piece, first, second):
    before, behind, far_low, far_high = ring(piece, first)
    low = jnp.concatenate([piece, before], 0)
    high = jnp.concatenate([behind, far_low, far_high], 0)

    def pass_on(part, step):
        return lax.ppermute(part, "seq", second(step))

    low_before, high_behind = pass_on(low, 1), pass_on(high, -1)
    low_behind, high_before = pass_on(low, -1), pass_on(high, 1)
    low_far, high_far = pass_on(low_before, 1), pass_on(high_behind, -1)
    return [low, high, low_before, high_before, low_behind, high_behind, low_far, high_far]


def attend_first_kernel(kmax, tab, q_ref, *refs):
    parts, (o_ref, k_out, v_out), (k_all, v_all, sem) = refs[: 2 * PARTS], refs[2 * PARTS : -3], refs[-3:]
    copies = []
    for some, whole in ((parts[:PARTS], k_all), (parts[PARTS:], v_all)):
        at = 0
        for part in some:
            copies.append(pltpu.make_async_copy(part, whole.at[pl.ds(at, part.shape[0])], sem.at[len(copies)]))
            at += part.shape[0]
    for copy in copies:
        copy.start()
    for copy in copies:
        copy.wait()
    keep = [
        pltpu.make_async_copy(k_all, k_out, sem.at[2 * PARTS]),
        pltpu.make_async_copy(v_all, v_out, sem.at[2 * PARTS + 1]),
    ]
    for copy in keep:
        copy.start()
    attend_kernel(kmax, tab, q_ref, k_all, v_all, o_ref)
    for copy in keep:
        copy.wait()


def attend_kernel(kmax, tab, q_ref, k_all, v_all, o_ref):
    heads = q_ref.shape[1] // HEAD_DIM
    units = q_ref.shape[0] // BLOCK * heads
    counts_at, keys_at, values_at = units, 2 * units, 2 * units + units * kmax
    scale = HEAD_DIM ** -0.5 * math.log2(math.e)
    rows = lax.broadcasted_iota(jnp.int32, (BLOCK, BLOCK), 0)
    cols = lax.broadcasted_iota(jnp.int32, (BLOCK, BLOCK), 1)
    causal = rows >= cols

    def block_of(ref, slot):
        return ref[pl.ds(pl.multiple_of(slot * BLOCK, BLOCK), BLOCK), :]

    def unit_scores(unit, pairs):
        head, local = unit % heads, unit // heads
        q = q_ref[
            pl.ds(pl.multiple_of(local * BLOCK, BLOCK), BLOCK),
            pl.ds(pl.multiple_of(head * HEAD_DIM, HEAD_DIM), HEAD_DIM),
        ]
        count = tab[counts_at + unit]
        scores = []
        for pair in range(pairs):
            two = jnp.concatenate(
                [block_of(k_all, tab[keys_at + unit * kmax + 2 * pair + i]) for i in range(2)], 0
            )
            both = lax.dot_general(q, two, (((1,), (1,)), ((), ())), preferred_element_type=jnp.float32)
            for i in range(2):
                j = 2 * pair + i
                one = both[:, i * BLOCK : (i + 1) * BLOCK]
                if j == 0:
                    one = jnp.where(causal, one, NEG)
                else:
                    one = one + jnp.where(j < count, 0.0, NEG).astype(jnp.float32)
                scores.append(one)
        return scores

    def unit_weights(scores):
        top = functools.reduce(jnp.maximum, scores)
        top = jnp.max(top, axis=1, keepdims=True)
        weights = [jnp.exp2((one - top) * scale) for one in scores]
        total = functools.reduce(jnp.add, weights)
        total = jnp.sum(total, axis=1, keepdims=True)
        return [one.astype(jnp.bfloat16) for one in weights], total

    def unit_finish(unit, weights, total):
        head, local = unit % heads, unit // heads
        values = jnp.concatenate(
            [block_of(v_all, tab[values_at + unit * kmax + j]) for j in range(len(weights))], 0
        )
        acc = jnp.dot(jnp.concatenate(weights, 1), values, preferred_element_type=jnp.float32)
        o_ref[
            pl.ds(pl.multiple_of(local * BLOCK, BLOCK), BLOCK),
            pl.ds(pl.multiple_of(head * HEAD_DIM, HEAD_DIM), HEAD_DIM),
        ] = (acc / total).astype(jnp.bfloat16)

    def step(group, carry):
        members = [tab[2 * group + i] for i in range(2)]
        most = jnp.maximum(tab[counts_at + members[0]], tab[counts_at + members[1]])
        need = (most + 1) // 2
        fewer = 0
        for pairs in VARIANTS:

            @pl.when((need > fewer) & (need <= pairs))
            def _():
                scores = [unit_scores(unit, pairs) for unit in members]
                ready = [unit_weights(one) for one in scores]
                for unit, (weights, total) in zip(members, ready):
                    unit_finish(unit, weights, total)

            fewer = pairs
        return carry

    lax.fori_loop(0, units // 2, step, 0)


def in_hbm(array):
    return pltpu.with_memory_space_constraint(array, pltpu.HBM)


def in_vmem(array):
    return pltpu.with_memory_space_constraint(array, pltpu.VMEM)


def attend(table, queries, kmax, k_parts, v_parts):
    rows, width = queries.shape
    tokens = sum(part.shape[0] for part in k_parts)
    vmem = pl.BlockSpec(memory_space=pltpu.VMEM)
    smem = pl.BlockSpec(memory_space=pltpu.SMEM)
    pairs = rows // BLOCK * (width // HEAD_DIM) * kmax // 2
    declared = cost(pairs * 4 * BLOCK * BLOCK * HEAD_DIM, 4 * tokens * HEAD_DIM + 4 * rows * width)
    gathered = len(k_parts) > 1
    params = pltpu.CompilerParams(vmem_limit_bytes=(20 if gathered else 8) << 20)
    out = jax.ShapeDtypeStruct((rows, width), jnp.bfloat16)
    if gathered:
        hbm = pl.BlockSpec(memory_space=pltpu.HBM)
        whole = pltpu.HBM((tokens, HEAD_DIM), jnp.bfloat16)
        held = pltpu.VMEM((tokens, HEAD_DIM), jnp.bfloat16)
        return pl.pallas_call(
            functools.partial(attend_first_kernel, kmax),
            out_shape=[out, whole, whole],
            in_specs=[smem, vmem] + [hbm] * (2 * PARTS),
            out_specs=[vmem, hbm, hbm],
            scratch_shapes=[held, held, pltpu.SemaphoreType.DMA((2 * PARTS + 2,))],
            compiler_params=params,
            cost_estimate=declared,
            name="attend_first",
        )(table, queries, *map(in_hbm, k_parts), *map(in_hbm, v_parts))
    return pl.pallas_call(
        functools.partial(attend_kernel, kmax),
        out_shape=out,
        in_specs=[smem, vmem, vmem, vmem],
        out_specs=vmem,
        compiler_params=params,
        cost_estimate=declared,
        name="attend",
    )(table, queries, in_vmem(k_parts[0]), in_vmem(v_parts[0]))


def tables(key_blocks, block_counts, seq_index, local_blocks):
    heads, _, kmax = key_blocks.shape
    start = seq_index * local_blocks
    lists = lax.dynamic_slice_in_dim(key_blocks, start, local_blocks, 1)
    counts = lax.dynamic_slice_in_dim(block_counts, start, local_blocks, 1)
    source = lists // local_blocks
    within = lists % local_blocks

    def place(step):
        step = step % SIDE
        return jnp.where(step == 0, 0, jnp.where(step == SIDE - 1, 1, jnp.where(step == 1, 2, 3)))

    z_place = place(source // SIDE - seq_index // SIDE)
    x_place = place(source % SIDE - seq_index % SIDE)
    key_at = (z_place * SIDE + x_place) * local_blocks + within
    value_at = (x_place * SIDE + z_place) * local_blocks + within
    counts, key_at, value_at = (jnp.moveaxis(one, 1, 0) for one in (counts, key_at, value_at))
    counts, key_at, value_at = (one.reshape(-1) for one in (counts, key_at, value_at))
    chunk = [index for index, blocks in enumerate(CHUNKS) for _ in range(blocks * heads)]
    order = jnp.argsort(counts + (kmax + 1) * jnp.array(chunk, jnp.int32)).astype(jnp.int32)
    out, at = [], 0
    for blocks in CHUNKS:
        units = slice(at, at + blocks * heads)
        slots = slice(at * kmax, (at + blocks * heads) * kmax)
        out.append(jnp.concatenate([order[units] - at, counts[units], key_at[slots], value_at[slots]], 0))
        at += blocks * heads
    return lax.optimization_barrier(out)


def product_kernel(sends, owns, cols, *refs):
    ins, refs = refs[: 2 * (sends + owns)], refs[2 * (sends + owns) :]
    w_ref, v_ref = refs[:2]
    outs, (both, w_buf, sem), lefts = refs[2 : 2 + 4 * sends + owns], refs[-3:], refs[2 + 4 * sends + owns : -3]
    depth = ins[0].shape[1]
    width = w_buf.shape[2]
    strip = 2 * depth // sem.shape[1]
    first = 0 if sends else 3

    def copies(k):
        source = pl.ds(pl.multiple_of(cols[first + k] * width, width), width)
        return [
            pltpu.make_async_copy(
                one.at[pl.ds(i * strip, strip), source],
                w_buf.at[k, pl.ds(which * depth + i * strip, strip), :],
                sem.at[k, which * (depth // strip) + i],
            )
            for which, one in enumerate((w_ref, v_ref))
            for i in range(depth // strip)
        ]

    for k in range(3 * sends + owns):
        for copy in copies(k):
            copy.start()
    for left, a_ref, b_ref in zip(lefts, ins[::2], ins[1::2]):
        left[:, :depth] = a_ref[...]
        left[:, depth:] = b_ref[...]

    def run(k, carry):
        for copy in copies(k):
            copy.wait()
        half = both.shape[0] // 2
        both[...] = jnp.dot(lefts[0][...], w_buf[k], preferred_element_type=jnp.float32)

        @pl.when(k == 0)
        def _():
            outs[0][:half, :] = both[:half, :].astype(jnp.bfloat16)
            outs[1][:half, :] = both[half:, :].astype(jnp.bfloat16)

        @pl.when(k == 1)
        def _():
            outs[0][half:, :] = both[half:, :].astype(jnp.bfloat16)
            outs[2][...] = both[:half, :]

        @pl.when(k == 2)
        def _():
            outs[1][half:, :] = both[:half, :].astype(jnp.bfloat16)
            outs[3][...] = both[half:, :]

        return carry

    if sends:
        lax.fori_loop(0, 3, run, 0)
    if owns:
        for copy in copies(3 * sends):
            copy.wait()
        outs[-1][...] = jnp.dot(lefts[-1][...], w_buf[3 * sends], preferred_element_type=jnp.float32)


def product(cols, now, before, weight, theirs):
    depth = weight.shape[0]
    width = weight.shape[1] // (SIDE * CORES)
    sends, owns = int(now is not None), int(before is not None)
    ins = (now or ()) + (before or ())
    rows = [one.shape[0] for one in ins[::2]]
    shapes = []
    if sends:
        shapes += [((rows[0], width), jnp.bfloat16)] * 2 + [((rows[0] // 2, width), jnp.float32)] * 2
    if owns:
        shapes += [((rows[-1], width), jnp.float32)]
    vmem = pl.BlockSpec(memory_space=pltpu.VMEM)
    hbm = pl.BlockSpec(memory_space=pltpu.HBM)
    steps = 3 * sends + owns
    return pl.pallas_call(
        functools.partial(product_kernel, sends, owns),
        out_shape=[jax.ShapeDtypeStruct(s, d) for s, d in shapes],
        in_specs=[pl.BlockSpec(memory_space=pltpu.SMEM)] + [vmem] * len(ins) + [hbm] * 2,
        out_specs=[vmem] * len(shapes),
        scratch_shapes=[pltpu.VMEM((one, 2 * depth), jnp.bfloat16) for one in rows]
        + [
            pltpu.VMEM((rows[0], width), jnp.float32),
            pltpu.VMEM((steps, 2 * depth, width), jnp.bfloat16),
            pltpu.SemaphoreType.DMA((steps, 8)),
        ],
        compiler_params=pltpu.CompilerParams(vmem_limit_bytes=(12 + 4 * steps) << 20),
        cost_estimate=cost(
            4 * rows[0] * depth * width * steps, 8 * rows[0] * width + 4 * depth * width * steps
        ),
        name="product",
    )(cols, *ins, in_hbm(weight), in_hbm(theirs))


def cost(flops, bytes_accessed):
    return pl.CostEstimate(flops=flops * 8 // COST, bytes_accessed=bytes_accessed // COST, transcendentals=0)


def after(value, *others):
    return lax.optimization_barrier((value,) + others)[0]


def body(queries, keys, values, key_blocks, block_counts, out_weight):
    tokens = queries.shape[0]
    seq_index = lax.axis_index("seq")
    tensor_index = lax.axis_index("tensor")
    y, core = tensor_index // CORES, tensor_index % CORES
    kmax = key_blocks.shape[2]
    k_parts = gather(keys, along_x, along_z)
    v_parts = gather(values, along_z, along_x)
    plans = tables(key_blocks, block_counts, seq_index, tokens // BLOCK)

    cols = jnp.stack([(y + step) % SIDE * CORES + core for step in ORDER]).astype(jnp.int32)
    theirs = lax.ppermute(after(out_weight, *k_parts[:2], *v_parts[:2]), "tensor", other_core())

    def send(piece, step):
        return lax.ppermute(piece, "tensor", along_y(step))

    def second(up, down, up_rest, down_rest):
        half = up_rest.shape[0]
        low = (up_rest + up[:half].astype(jnp.float32)).astype(jnp.bfloat16)
        high = (down_rest + down[:half].astype(jnp.float32)).astype(jnp.bfloat16)
        return low, high

    def finish(own, up, down, up_low, down_high):
        half = own.shape[0] // 2
        low = own[:half] + up_low.astype(jnp.float32) + down[half:].astype(jnp.float32)
        high = own[half:] + up[half:].astype(jnp.float32) + down_high.astype(jnp.float32)
        return [low.astype(jnp.bfloat16), high.astype(jnp.bfloat16)]

    results = []
    at = 0
    before, settled = None, ()
    for blocks, plan in zip(CHUNKS, plans):
        some = queries[at : at + blocks * BLOCK]
        at += blocks * BLOCK
        if before is None:
            attended, key_all, value_all = attend(plan, some, kmax, k_parts, v_parts)
        else:
            attended = attend(after(plan, up_rest, *settled), some, kmax, [key_all], [value_all])
        swapped = lax.ppermute(attended, "tensor", other_core())
        if before is None:
            made = product(cols, (attended, swapped), None, out_weight, theirs)
        else:
            low, high = second(up, down, up_rest, down_rest)
            pair = after(attended, low, high), swapped
            low, high = send(low, 1), send(high, -1)
            *made, own = product(cols, pair, before, out_weight, theirs)
            results += finish(own, up, down, low, high)
            settled = low, high
        up, down, up_rest, down_rest = made
        up, down = send(up, 1), send(down, -1)
        before = attended, swapped
    (own,) = product(cols, None, before, out_weight, theirs)
    low, high = second(up, down, up_rest, down_rest)
    results += finish(own, up, down, send(low, 1), send(high, -1))
    return jnp.concatenate(results, 0)


def solution(mesh):
    placed = (
        P("seq", "tensor"),
        P("seq", "tensor"),
        P("seq", "tensor"),
        P("tensor", None, None),
        P("tensor", None),
        P("tensor", None),
    )
    return jax.shard_map(
        body, mesh=mesh, in_specs=placed, out_specs=P("seq", "tensor"), check_vma=False
    )
```

profile of v0, /device:TPU:96, one launch (start us, length us, event | category | flops | bytes accessed | tf_op | source)
XLA Modules:
  0.0 184.7 jit_solution(10537664101854751389)
XLA Ops:
  0.0 2.0 %collective-permute-start.11 = (bf16[1024,128]{1,0:T(8,128)(2,1)}, bf16[1024,128]{1,0:T(8,128)(2,1)S(1)}, u32[]{:S(2)}, u32[]{:S(2)}) collective-permute-start(bf16[1024,128]{1,0:T(8,128)(2,1)} %param.9), channel_id=1, source_target_pairs={{0,96},{8,104},{16,112},{24,120},{32,0},{40,8},{48,16},{56,24},{64... | collective-permute-start | bytes 786440 | tf_op jit(solution)/shard_map/ppermute | solution.py:42
  2.0 1.5 collective-permute-start
  3.5 1.7 collective-permute-start.1
  5.3 1.0 constant_dynamic-update-slice_fusion.6
  6.2 1.0 constant_dynamic-update-slice_fusion.1
  7.2 1.0 collective-permute-done.10
  8.3 1.6 collective-permute-start.12
  10.9 1.1 collective-permute-start.2
  12.0 2.3 %collective-permute-start.3 = (bf16[512,128]{1,0:T(8,128)(2,1)S(1)}, bf16[512,128]{1,0:T(8,128)(2,1)S(1)}, u32[]{:S(2)}, u32[]{:S(2)}) collective-permute-start(bf16[512,128]{1,0:T(8,128)(2,1)S(1)} %slice.191), channel_id=1, source_target_pairs={{0,24},{8,0},{16,8},{24,16},{32,56},{40,32},{48,40},{56,48},{64,88... | collective-permute-start | bytes 393224 | tf_op jit(solution)/shard_map/ppermute | solution.py:44
  14.3 0.7 constant_dynamic-update-slice_fusion.9
  15.9 0.8 constant_dynamic-update-slice_fusion.8
  18.9 2.0 %sort.17 = (s32[64]{0:T(128)}, s32[64]{0:T(128)S(1)}) sort(s32[64]{0:T(128)S(1)} %reshape.16, s32[64]{0:T(128)S(1)} %iota.4), dimensions={0}, to_apply=%region_0.1 | sort | flops 384 | bytes 1024 | tf_op jit(solution)/shard_map/jit(argsort)/sort | solution.py:221
  21.0 0.9 collective-permute-start.14
  21.9 2.4 %collective-permute-start.4 = (bf16[2048,128]{1,0:T(8,128)(2,1)S(1)}, bf16[2048,128]{1,0:T(8,128)(2,1)}, u32[]{:S(2)}, u32[]{:S(2)}) collective-permute-start(bf16[2048,128]{1,0:T(8,128)(2,1)S(1)} %constant_dynamic-update-slice_fusion.refs_0_), channel_id=1, source_target_pairs={{0,32},{8,40},{16,48},{24,56},{32,64},{40,72},{48,80},{56,88},{64,... | collective-permute-start | bytes 1572872 | tf_op jit(solution)/shard_map/ppermute | solution.py:54
  24.2 2.2 %collective-permute-start.16 = (bf16[2048,128]{1,0:T(8,128)(2,1)S(1)}, bf16[2048,128]{1,0:T(8,128)(2,1)S(1)}, u32[]{:S(2)}, u32[]{:S(2)}) collective-permute-start(bf16[2048,128]{1,0:T(8,128)(2,1)S(1)} %constant_dynamic-update-slice_fusion.5.refs_8_), channel_id=1, source_target_pairs={{0,24},{8,0},{16,8},{24,16},{32,56},{40,32},{48,40},{56,48},{64,88... | collective-permute-start | bytes 1572872 | tf_op jit(solution)/shard_map/ppermute | solution.py:54
  27.1 9.5 %collective-permute-done.14.refs_10_ = bf16[2048,128]{1,0:T(8,128)(2,1)} collective-permute-done((bf16[2048,128]{1,0:T(8,128)(2,1)S(1)}, bf16[2048,128]{1,0:T(8,128)(2,1)}, u32[]{:S(2)}, u32[]{:S(2)}) %collective-permute-start.14) | collective-permute-done | bytes 524320 | tf_op jit(solution)/shard_map/ppermute | solution.py:54
  36.6 1.3 collective-permute-start.17
  38.3 1.2 collective-permute-start.15
  39.5 1.6 collective-permute-done.6.refs_4_
  41.1 0.8 collective-permute-start.5
  42.1 8.3 %collective-permute-done.17.refs_13_ = bf16[2048,128]{1,0:T(8,128)(2,1)} collective-permute-done((bf16[2048,128]{1,0:T(8,128)(2,1)}, bf16[2048,128]{1,0:T(8,128)(2,1)}, u32[]{:S(2)}, u32[]{:S(2)}) %collective-permute-start.17) | collective-permute-done | bytes 524320 | tf_op jit(solution)/shard_map/ppermute | solution.py:54
  50.5 2.2 %collective-permute-done.7.refs_5_ = bf16[2048,128]{1,0:T(8,128)(2,1)} collective-permute-done((bf16[2048,128]{1,0:T(8,128)(2,1)}, bf16[2048,128]{1,0:T(8,128)(2,1)}, u32[]{:S(2)}, u32[]{:S(2)}) %collective-permute-start.7) | collective-permute-done | bytes 524320 | tf_op jit(solution)/shard_map/ppermute | solution.py:54
  52.7 1.0 collective-permute-start.8
  53.7 2.2 %collective-permute-start.19 = (bf16[2048,128]{1,0:T(8,128)(2,1)}, bf16[2048,128]{1,0:T(8,128)(2,1)}, u32[]{:S(2)}, u32[]{:S(2)}) collective-permute-start(bf16[2048,128]{1,0:T(8,128)(2,1)} %collective-permute-done.17.refs_13_), channel_id=1, source_target_pairs={{0,24},{8,0},{16,8},{24,16},{32,56},{40,32},{48,40},{56,48},{64,88... | collective-permute-start | bytes 1572872 | tf_op jit(solution)/shard_map/ppermute | solution.py:54
  58.8 5.9 %collective-permute-done.18.refs_14_ = bf16[2048,128]{1,0:T(8,128)(2,1)} collective-permute-done((bf16[2048,128]{1,0:T(8,128)(2,1)}, bf16[2048,128]{1,0:T(8,128)(2,1)}, u32[]{:S(2)}, u32[]{:S(2)}) %collective-permute-start.18) | collective-permute-done | bytes 524320 | tf_op jit(solution)/shard_map/ppermute | solution.py:54
  65.4 0.7 collective-permute-done.19.refs_15_
  66.1 3.2 %collective-permute-done.9.refs_7_ = bf16[2048,128]{1,0:T(8,128)(2,1)} collective-permute-done((bf16[2048,128]{1,0:T(8,128)(2,1)}, bf16[2048,128]{1,0:T(8,128)(2,1)}, u32[]{:S(2)}, u32[]{:S(2)}) %collective-permute-start.9) | collective-permute-done | bytes 524320 | tf_op jit(solution)/shard_map/ppermute | solution.py:54
  69.3 10.5 %attend_first.1 = (bf16[384,1024]{1,0:T(8,128)(2,1)S(1)}, bf16[16384,128]{1,0:T(8,128)(2,1)}, bf16[16384,128]{1,0:T(8,128)(2,1)}) custom-call(s32[816]{0:T(1024)S(1)} %get-tuple-element.33.tab, bf16[384,1024]{1,0:T(8,128)(2,1)S(1)} %get-tuple-element.62.q_ref, bf16[2048,128]{1,0:T(8,128)(2,1)} %copy-done.4, ...), custom_call_target="tpu_custom_call" | custom-call | flops 6442450944 | bytes 4980736 | tf_op jit(solution)/shard_map/attend_first/pallas_call | solution.py:181
  80.1 2.1 %collective-permute-done.20.refs_1_.refs_3_ = bf16[384,1024]{1,0:T(8,128)(2,1)S(1)} collective-permute-done((bf16[384,1024]{1,0:T(8,128)(2,1)S(1)}, bf16[384,1024]{1,0:T(8,128)(2,1)S(1)}, u32[]{:S(2)}, u32[]{:S(2)}) %collective-permute-start.20) | collective-permute-done | bytes 786464 | tf_op jit(solution)/shard_map/ppermute | solution.py:369
  82.2 8.6 %product.4 = (bf16[384,1024]{1,0:T(8,128)(2,1)S(1)}, bf16[384,1024]{1,0:T(8,128)(2,1)S(1)}, f32[192,1024]{1,0:T(8,128)S(1)}, f32[192,1024]{1,0:T(8,128)S(1)}) custom-call(s32[4]{0:T(128)S(1)} %pad_add_fusion.3.cols, bf16[384,1024]{1,0:T(8,128)(2,1)S(1)} %get-tuple-element.34.refs_0_.refs_2_, bf16[384,1024]{1,0:T(8,128)(2,1)S(1)} %collective-permute-done.20.refs_1_.refs_3_, ...), custom_call_target="tpu_custom_call" | custom-call | flops 19327352832 | bytes 7864320 | tf_op jit(solution)/shard_map/product/pallas_call | solution.py:304
  90.8 4.7 %collective-permute-start.23 = (bf16[384,1024]{1,0:T(8,128)(2,1)S(1)}, bf16[384,1024]{1,0:T(8,128)(2,1)S(1)}, u32[]{:S(2)}, u32[]{:S(2)}) collective-permute-start(bf16[384,1024]{1,0:T(8,128)(2,1)S(1)} %get-tuple-element.42), channel_id=1, source_target_pairs={{0,6},{1,7},{2,0},{3,1},{4,2},{5,3},{6,4},{7,5},{8,14},{9,15},{10,... | collective-permute-start | bytes 2359304 | tf_op jit(solution)/shard_map/ppermute | solution.py:345
  95.5 7.7 %attend.2.refs_0_.refs_2_ = bf16[384,1024]{1,0:T(8,128)(2,1)S(1)} custom-call(s32[816]{0:T(1024)S(1)} %get-tuple-element.37.tab, bf16[384,1024]{1,0:T(8,128)(2,1)S(1)} %get-tuple-element.61.q_ref, bf16[16384,128]{1,0:T(8,128)(2,1)S(1)} %copy-done, bf16[16384,128]{1,0:T(8,128)(2,1)S(1)} %copy-done.1), custom_call_target="tpu_custom_call" | custom-call | flops 6442450944 | bytes 4980736 | tf_op jit(solution)/shard_map/attend/pallas_call | solution.py:191
  103.7 1.1 slice.171.q_ref
  104.8 7.9 %collective-permute-done.23 = bf16[384,1024]{1,0:T(8,128)(2,1)S(1)} collective-permute-done((bf16[384,1024]{1,0:T(8,128)(2,1)S(1)}, bf16[384,1024]{1,0:T(8,128)(2,1)S(1)}, u32[]{:S(2)}, u32[]{:S(2)}) %collective-permute-start.23) | collective-permute-done | bytes 786464 | tf_op jit(solution)/shard_map/ppermute | solution.py:345
  112.7 3.8 %collective-permute-start.26 = (bf16[192,1024]{1,0:T(8,128)(2,1)S(1)}, bf16[192,1024]{1,0:T(8,128)(2,1)S(1)}, u32[]{:S(2)}, u32[]{:S(2)}) collective-permute-start(bf16[192,1024]{1,0:T(8,128)(2,1)S(1)} %add_convert_fusion.6), channel_id=1, source_target_pairs={{0,6},{1,7},{2,0},{3,1},{4,2},{5,3},{6,4},{7,5},{8,14},{9,15},{10,... | collective-permute-start | bytes 1179656 | tf_op jit(solution)/shard_map/ppermute | solution.py:345
  116.9 10.4 %product.5 = (bf16[384,1024]{1,0:T(8,128)(2,1)S(1)}, bf16[384,1024]{1,0:T(8,128)(2,1)S(1)}, f32[192,1024]{1,0:T(8,128)S(1)}, f32[192,1024]{1,0:T(8,128)S(1)}, f32[384,1024]{1,0:T(8,128)S(1)}) custom-call(s32[4]{0:T(128)S(1)} %pad_add_fusion.3.cols, bf16[384,1024]{1,0:T(8,128)(2,1)S(1)} %attend.2.refs_0_.refs_2_, ...), custom_call_target="tpu_custom_call" | custom-call | flops 25769803776 | bytes 9961472 | tf_op jit(solution)/shard_map/product/pallas_call | solution.py:304
  127.4 3.3 %collective-permute-start.28 = (bf16[384,1024]{1,0:T(8,128)(2,1)S(1)}, bf16[384,1024]{1,0:T(8,128)(2,1)S(1)}, u32[]{:S(2)}, u32[]{:S(2)}) collective-permute-start(bf16[384,1024]{1,0:T(8,128)(2,1)S(1)} %get-tuple-element.50), channel_id=1, source_target_pairs={{0,6},{1,7},{2,0},{3,1},{4,2},{5,3},{6,4},{7,5},{8,14},{9,15},{10,... | collective-permute-start | bytes 2359304 | tf_op jit(solution)/shard_map/ppermute | solution.py:345
  130.7 5.8 %attend.3.refs_0_ = bf16[256,1024]{1,0:T(8,128)(2,1)S(1)} custom-call(s32[544]{0:T(1024)S(1)} %pad_add_fusion.2.tab, bf16[256,1024]{1,0:T(8,128)(2,1)S(1)} %slice.171.q_ref, bf16[16384,128]{1,0:T(8,128)(2,1)S(1)} %copy-done, bf16[16384,128]{1,0:T(8,128)(2,1)S(1)} %copy-done.1), custom_call_target="tpu_custom_call" | custom-call | flops 4294967296 | bytes 4718592 | tf_op jit(solution)/shard_map/attend/pallas_call | solution.py:191
  137.0 12.9 %collective-permute-done.27 = bf16[384,1024]{1,0:T(8,128)(2,1)S(1)} collective-permute-done((bf16[384,1024]{1,0:T(8,128)(2,1)S(1)}, bf16[384,1024]{1,0:T(8,128)(2,1)S(1)}, u32[]{:S(2)}, u32[]{:S(2)}) %collective-permute-start.27) | collective-permute-done | bytes 786464 | tf_op jit(solution)/shard_map/ppermute | solution.py:345
  150.2 3.3 %collective-permute-start.31 = (bf16[192,1024]{1,0:T(8,128)(2,1)S(1)}, bf16[192,1024]{1,0:T(8,128)(2,1)S(1)}, u32[]{:S(2)}, u32[]{:S(2)}) collective-permute-start(bf16[192,1024]{1,0:T(8,128)(2,1)S(1)} %add_convert_fusion.2), channel_id=1, source_target_pairs={{0,6},{1,7},{2,0},{3,1},{4,2},{5,3},{6,4},{7,5},{8,14},{9,15},{10,... | collective-permute-start | bytes 1179656 | tf_op jit(solution)/shard_map/ppermute | solution.py:345
  153.4 8.7 %product.6 = (bf16[256,1024]{1,0:T(8,128)(2,1)S(1)}, bf16[256,1024]{1,0:T(8,128)(2,1)S(1)}, f32[128,1024]{1,0:T(8,128)S(1)}, f32[128,1024]{1,0:T(8,128)S(1)}, f32[384,1024]{1,0:T(8,128)S(1)}) custom-call(s32[4]{0:T(128)S(1)} %pad_add_fusion.3.cols, bf16[256,1024]{1,0:T(8,128)(2,1)S(1)} %attend.3.refs_0_, ...), custom_call_target="tpu_custom_call" | custom-call | flops 17179869184 | bytes 9437184 | tf_op jit(solution)/shard_map/product/pallas_call | solution.py:304
  162.3 2.0 %collective-permute-start.32 = (bf16[256,1024]{1,0:T(8,128)(2,1)S(1)}, bf16[256,1024]{1,0:T(8,128)(2,1)S(1)}, u32[]{:S(2)}, u32[]{:S(2)}) collective-permute-start(bf16[256,1024]{1,0:T(8,128)(2,1)S(1)} %get-tuple-element.54), channel_id=1, source_target_pairs={{0,2},{1,3},{2,4},{3,5},{4,6},{5,7},{6,0},{7,1},{8,10},{9,11},{10,... | collective-permute-start | bytes 1572872 | tf_op jit(solution)/shard_map/ppermute | solution.py:345
  164.3 4.0 %product.7 = f32[256,1024]{1,0:T(8,128)S(1)} custom-call(s32[4]{0:T(128)S(1)} %pad_add_fusion.3.cols, bf16[256,1024]{1,0:T(8,128)(2,1)S(1)} %attend.3.refs_0_, bf16[256,1024]{1,0:T(8,128)(2,1)S(1)} %collective-permute-done.29.refs_1_, bf16[1024,8192]{1,0:T(8,128)(2,1)} %refs_2_.3, bf16[1024,8192]{1,0:T(8,128)(2,1)} %collective-permute-done.21.refs_3_.refs_5_), custom_call_target="tpu_custom_call" | custom-call | flops 4294967296 | bytes 3145728 | tf_op jit(solution)/shard_map/product/pallas_call | solution.py:304
  168.5 5.7 %collective-permute-done.34 = bf16[256,1024]{1,0:T(8,128)(2,1)S(1)} collective-permute-done((bf16[256,1024]{1,0:T(8,128)(2,1)S(1)}, bf16[256,1024]{1,0:T(8,128)(2,1)S(1)}, u32[]{:S(2)}, u32[]{:S(2)}) %collective-permute-start.34) | collective-permute-done | bytes 524320 | tf_op jit(solution)/shard_map/ppermute | solution.py:345
  174.8 1.7 collective-permute-start.33
  176.7 5.8 %collective-permute-done.33 = bf16[128,1024]{1,0:T(8,128)(2,1)S(1)} collective-permute-done((bf16[128,1024]{1,0:T(8,128)(2,1)S(1)}, bf16[128,1024]{1,0:T(8,128)(2,1)S(1)}, u32[]{:S(2)}, u32[]{:S(2)}) %collective-permute-start.33) | collective-permute-done | bytes 262176 | tf_op jit(solution)/shard_map/ppermute | solution.py:345
  182.6 1.3 copy-done.6
  183.9 0.8 fusion.9
  (121 shorter events, 12.1 us)
Async XLA Ops:
  0.0 8.3 %collective-permute-start.10 = (bf16[1024,128]{1,0:T(8,128)(2,1)}, bf16[1024,128]{1,0:T(8,128)(2,1)S(1)}, u32[]{:S(2)}, u32[]{:S(2)}) collective-permute-start(bf16[1024,128]{1,0:T(8,128)(2,1)} %param.9), channel_id=1, source_target_pairs={{0,32},{8,40},{16,48},{24,56},{32,64},{40,72},{48,80},{56,88},{64,... | collective-permute-start | bytes 786440 | tf_op jit(solution)/shard_map/ppermute | solution.py:41
  0.0 9.8 %collective-permute-start.11 = (bf16[1024,128]{1,0:T(8,128)(2,1)}, bf16[1024,128]{1,0:T(8,128)(2,1)S(1)}, u32[]{:S(2)}, u32[]{:S(2)}) collective-permute-start(bf16[1024,128]{1,0:T(8,128)(2,1)} %param.9), channel_id=1, source_target_pairs={{0,96},{8,104},{16,112},{24,120},{32,0},{40,8},{48,16},{56,24},{64... | collective-permute-start | bytes 786440 | tf_op jit(solution)/shard_map/ppermute | solution.py:42
  2.0 8.9 %collective-permute-start = (bf16[1024,128]{1,0:T(8,128)(2,1)}, bf16[1024,128]{1,0:T(8,128)(2,1)S(1)}, u32[]{:S(2)}, u32[]{:S(2)}) collective-permute-start(bf16[1024,128]{1,0:T(8,128)(2,1)} %param.8), channel_id=1, source_target_pairs={{0,8},{8,16},{16,24},{24,0},{32,40},{40,48},{48,56},{56,32},{64,72... | collective-permute-start | bytes 786440 | tf_op jit(solution)/shard_map/ppermute | solution.py:41
  3.5 8.5 %collective-permute-start.1 = (bf16[1024,128]{1,0:T(8,128)(2,1)}, bf16[1024,128]{1,0:T(8,128)(2,1)S(1)}, u32[]{:S(2)}, u32[]{:S(2)}) collective-permute-start(bf16[1024,128]{1,0:T(8,128)(2,1)} %param.8), channel_id=1, source_target_pairs={{0,24},{8,0},{16,8},{24,16},{32,56},{40,32},{48,40},{56,48},{64,88... | collective-permute-start | bytes 786440 | tf_op jit(solution)/shard_map/ppermute | solution.py:42
  7.2 11.5 %copy-start.7 = (s32[8,128]{1,0:T(8,128)S(1)}, s32[8,128]{1,0:T(8,128)}, u32[]{:S(2)}) copy-start(s32[8,128]{1,0:T(8,128)} %param.11) | copy-start | bytes 12292
  7.2 11.5 %copy-start.8 = (s32[8,8]{0,1:T(8,128)S(1)}, s32[8,8]{0,1:T(8,128)}, u32[]{:S(2)}) copy-start(s32[8,8]{0,1:T(8,128)} %constant.135) | copy-start | bytes 772
  7.2 19.2 %copy-start.3 = (s32[8,128,16]{1,2,0:T(8,128)S(1)}, s32[8,128,16]{1,2,0:T(8,128)}, u32[]{:S(2)}) copy-start(s32[8,128,16]{1,2,0:T(8,128)} %param.10) | copy-start | bytes 196612
  8.3 7.6 %collective-permute-start.12 = (bf16[512,128]{1,0:T(8,128)(2,1)S(1)}, bf16[512,128]{1,0:T(8,128)(2,1)S(1)}, u32[]{:S(2)}, u32[]{:S(2)}) collective-permute-start(bf16[512,128]{1,0:T(8,128)(2,1)S(1)} %slice.192), channel_id=1, source_target_pairs={{0,32},{8,40},{16,48},{24,56},{32,64},{40,72},{48,80},{56,88},{64,... | collective-permute-start | bytes 393224 | tf_op jit(solution)/shard_map/ppermute | solution.py:43
  9.9 6.8 %collective-permute-start.13 = (bf16[512,128]{1,0:T(8,128)(2,1)S(1)}, bf16[512,128]{1,0:T(8,128)(2,1)S(1)}, u32[]{:S(2)}, u32[]{:S(2)}) collective-permute-start(bf16[512,128]{1,0:T(8,128)(2,1)S(1)} %slice.193), channel_id=1, source_target_pairs={{0,96},{8,104},{16,112},{24,120},{32,0},{40,8},{48,16},{56,24},{64... | collective-permute-start | bytes 393224 | tf_op jit(solution)/shard_map/ppermute | solution.py:44
  10.9 6.4 %collective-permute-start.2 = (bf16[512,128]{1,0:T(8,128)(2,1)S(1)}, bf16[512,128]{1,0:T(8,128)(2,1)S(1)}, u32[]{:S(2)}, u32[]{:S(2)}) collective-permute-start(bf16[512,128]{1,0:T(8,128)(2,1)S(1)} %slice.190), channel_id=1, source_target_pairs={{0,8},{8,16},{16,24},{24,0},{32,40},{40,48},{48,56},{56,32},{64,72... | collective-permute-start | bytes 393224 | tf_op jit(solution)/shard_map/ppermute | solution.py:43
  12.0 6.0 %collective-permute-start.3 = (bf16[512,128]{1,0:T(8,128)(2,1)S(1)}, bf16[512,128]{1,0:T(8,128)(2,1)S(1)}, u32[]{:S(2)}, u32[]{:S(2)}) collective-permute-start(bf16[512,128]{1,0:T(8,128)(2,1)S(1)} %slice.191), channel_id=1, source_target_pairs={{0,24},{8,0},{16,8},{24,16},{32,56},{40,32},{48,40},{56,48},{64,88... | collective-permute-start | bytes 393224 | tf_op jit(solution)/shard_map/ppermute | solution.py:44
  15.1 43.6 %copy-start.2 = (bf16[1024,1024]{1,0:T(8,128)(2,1)S(1)}, bf16[1024,1024]{1,0:T(8,128)(2,1)}, u32[]{:S(2)}) copy-start(bf16[1024,1024]{1,0:T(8,128)(2,1)} %param.7) | copy-start | bytes 6291460
  15.8 26.1 %copy-start.5 = (bf16[2048,128]{1,0:T(8,128)(2,1)}, bf16[2048,128]{1,0:T(8,128)(2,1)S(1)}, u32[]{:S(2)}) copy-start(bf16[2048,128]{1,0:T(8,128)(2,1)S(1)} %constant_dynamic-update-slice_fusion.5.refs_8_) | copy-start | bytes 1572868
  15.9 42.9 %copy-start.4 = (bf16[2048,128]{1,0:T(8,128)(2,1)}, bf16[2048,128]{1,0:T(8,128)(2,1)S(1)}, u32[]{:S(2)}) copy-start(bf16[2048,128]{1,0:T(8,128)(2,1)S(1)} %constant_dynamic-update-slice_fusion.refs_0_) | copy-start | bytes 1572868
  18.7 63.5 %collective-permute-start.21 = (bf16[1024,8192]{1,0:T(8,128)(2,1)}, bf16[1024,8192]{1,0:T(8,128)(2,1)}, u32[]{:S(2)}, u32[]{:S(2)}) collective-permute-start(bf16[1024,8192]{1,0:T(8,128)(2,1)} %refs_2_.3), channel_id=1, source_target_pairs={{0,1},{1,0},{2,3},{3,2},{4,5},{5,4},{6,7},{7,6},{8,9},{9,8},{10,11... | collective-permute-start | bytes 50331656 | tf_op jit(solution)/shard_map/ppermute | solution.py:342
  21.0 15.6 %collective-permute-start.14 = (bf16[2048,128]{1,0:T(8,128)(2,1)S(1)}, bf16[2048,128]{1,0:T(8,128)(2,1)}, u32[]{:S(2)}, u32[]{:S(2)}) collective-permute-start(bf16[2048,128]{1,0:T(8,128)(2,1)S(1)} %constant_dynamic-update-slice_fusion.5.refs_8_), channel_id=1, source_target_pairs={{0,8},{8,16},{16,24},{24,0},{32,40},{40,48},{48,56},{56,32},{64,72... | collective-permute-start | bytes 1572872 | tf_op jit(solution)/shard_map/ppermute | solution.py:54
  21.9 16.0 %collective-permute-start.4 = (bf16[2048,128]{1,0:T(8,128)(2,1)S(1)}, bf16[2048,128]{1,0:T(8,128)(2,1)}, u32[]{:S(2)}, u32[]{:S(2)}) collective-permute-start(bf16[2048,128]{1,0:T(8,128)(2,1)S(1)} %constant_dynamic-update-slice_fusion.refs_0_), channel_id=1, source_target_pairs={{0,32},{8,40},{16,48},{24,56},{32,64},{40,72},{48,80},{56,88},{64,... | collective-permute-start | bytes 1572872 | tf_op jit(solution)/shard_map/ppermute | solution.py:54
  24.2 14.1 %collective-permute-start.16 = (bf16[2048,128]{1,0:T(8,128)(2,1)S(1)}, bf16[2048,128]{1,0:T(8,128)(2,1)S(1)}, u32[]{:S(2)}, u32[]{:S(2)}) collective-permute-start(bf16[2048,128]{1,0:T(8,128)(2,1)S(1)} %constant_dynamic-update-slice_fusion.5.refs_8_), channel_id=1, source_target_pairs={{0,24},{8,0},{16,8},{24,16},{32,56},{40,32},{48,40},{56,48},{64,88... | collective-permute-start | bytes 1572872 | tf_op jit(solution)/shard_map/ppermute | solution.py:54
  26.4 14.7 %collective-permute-start.6 = (bf16[2048,128]{1,0:T(8,128)(2,1)S(1)}, bf16[2048,128]{1,0:T(8,128)(2,1)S(1)}, u32[]{:S(2)}, u32[]{:S(2)}) collective-permute-start(bf16[2048,128]{1,0:T(8,128)(2,1)S(1)} %constant_dynamic-update-slice_fusion.refs_0_), channel_id=1, source_target_pairs={{0,96},{8,104},{16,112},{24,120},{32,0},{40,8},{48,16},{56,24},{64... | collective-permute-start | bytes 1572872 | tf_op jit(solution)/shard_map/ppermute | solution.py:54
  36.6 13.9 %collective-permute-start.17 = (bf16[2048,128]{1,0:T(8,128)(2,1)}, bf16[2048,128]{1,0:T(8,128)(2,1)}, u32[]{:S(2)}, u32[]{:S(2)}) collective-permute-start(bf16[2048,128]{1,0:T(8,128)(2,1)} %constant_dynamic-update-slice_fusion.7.refs_9_), channel_id=1, source_target_pairs={{0,24},{8,0},{16,8},{24,16},{32,56},{40,32},{48,40},{56,48},{64,88... | collective-permute-start | bytes 1572872 | tf_op jit(solution)/shard_map/ppermute | solution.py:54
  37.9 14.8 %collective-permute-start.7 = (bf16[2048,128]{1,0:T(8,128)(2,1)}, bf16[2048,128]{1,0:T(8,128)(2,1)}, u32[]{:S(2)}, u32[]{:S(2)}) collective-permute-start(bf16[2048,128]{1,0:T(8,128)(2,1)} %constant_dynamic-update-slice_fusion.2.refs_1_), channel_id=1, source_target_pairs={{0,96},{8,104},{16,112},{24,120},{32,0},{40,8},{48,16},{56,24},{64... | collective-permute-start | bytes 1572872 | tf_op jit(solution)/shard_map/ppermute | solution.py:54
  38.3 18.0 %copy-start.9 = (bf16[2048,128]{1,0:T(8,128)(2,1)}, bf16[2048,128]{1,0:T(8,128)(2,1)S(1)}, u32[]{:S(2)}) copy-start(bf16[2048,128]{1,0:T(8,128)(2,1)S(1)} %collective-permute-done.16.refs_12_) | copy-start | bytes 1572868
  38.3 15.4 %collective-permute-start.15 = (bf16[2048,128]{1,0:T(8,128)(2,1)}, bf16[2048,128]{1,0:T(8,128)(2,1)S(1)}, u32[]{:S(2)}, u32[]{:S(2)}) collective-permute-start(bf16[2048,128]{1,0:T(8,128)(2,1)} %constant_dynamic-update-slice_fusion.7.refs_9_), channel_id=1, source_target_pairs={{0,8},{8,16},{16,24},{24,0},{32,40},{40,48},{48,56},{56,32},{64,72... | collective-permute-start | bytes 1572872 | tf_op jit(solution)/shard_map/ppermute | solution.py:54
  41.1 15.1 %copy-start.10 = (bf16[2048,128]{1,0:T(8,128)(2,1)}, bf16[2048,128]{1,0:T(8,128)(2,1)S(1)}, u32[]{:S(2)}) copy-start(bf16[2048,128]{1,0:T(8,128)(2,1)S(1)} %collective-permute-done.6.refs_4_) | copy-start | bytes 1572868
  41.1 14.8 %collective-permute-start.5 = (bf16[2048,128]{1,0:T(8,128)(2,1)}, bf16[2048,128]{1,0:T(8,128)(2,1)S(1)}, u32[]{:S(2)}, u32[]{:S(2)}) collective-permute-start(bf16[2048,128]{1,0:T(8,128)(2,1)} %constant_dynamic-update-slice_fusion.2.refs_1_), channel_id=1, source_target_pairs={{0,32},{8,40},{16,48},{24,56},{32,64},{40,72},{48,80},{56,88},{64,... | collective-permute-start | bytes 1572872 | tf_op jit(solution)/shard_map/ppermute | solution.py:54
  50.5 14.2 %collective-permute-start.18 = (bf16[2048,128]{1,0:T(8,128)(2,1)}, bf16[2048,128]{1,0:T(8,128)(2,1)}, u32[]{:S(2)}, u32[]{:S(2)}) collective-permute-start(bf16[2048,128]{1,0:T(8,128)(2,1)} %collective-permute-done.14.refs_10_), channel_id=1, source_target_pairs={{0,8},{8,16},{16,24},{24,0},{32,40},{40,48},{48,56},{56,32},{64,72... | collective-permute-start | bytes 1572872 | tf_op jit(solution)/shard_map/ppermute | solution.py:54
  52.7 12.7 %collective-permute-start.8 = (bf16[2048,128]{1,0:T(8,128)(2,1)}, bf16[2048,128]{1,0:T(8,128)(2,1)}, u32[]{:S(2)}, u32[]{:S(2)}) collective-permute-start(bf16[2048,128]{1,0:T(8,128)(2,1)} %collective-permute-done.4.refs_2_), channel_id=1, source_target_pairs={{0,32},{8,40},{16,48},{24,56},{32,64},{40,72},{48,80},{56,88},{64,... | collective-permute-start | bytes 1572872 | tf_op jit(solution)/shard_map/ppermute | solution.py:54
  53.7 2.6 %copy-start.11 = (bf16[2048,128]{1,0:T(8,128)(2,1)}, bf16[2048,128]{1,0:T(8,128)(2,1)S(1)}, u32[]{:S(2)}) copy-start(bf16[2048,128]{1,0:T(8,128)(2,1)S(1)} %collective-permute-done.15.refs_11_) | copy-start | bytes 1572868
  53.7 12.4 %collective-permute-start.19 = (bf16[2048,128]{1,0:T(8,128)(2,1)}, bf16[2048,128]{1,0:T(8,128)(2,1)}, u32[]{:S(2)}, u32[]{:S(2)}) collective-permute-start(bf16[2048,128]{1,0:T(8,128)(2,1)} %collective-permute-done.17.refs_13_), channel_id=1, source_target_pairs={{0,24},{8,0},{16,8},{24,16},{32,56},{40,32},{48,40},{56,48},{64,88... | collective-permute-start | bytes 1572872 | tf_op jit(solution)/shard_map/ppermute | solution.py:54
  56.0 13.3 %collective-permute-start.9 = (bf16[2048,128]{1,0:T(8,128)(2,1)}, bf16[2048,128]{1,0:T(8,128)(2,1)}, u32[]{:S(2)}, u32[]{:S(2)}) collective-permute-start(bf16[2048,128]{1,0:T(8,128)(2,1)} %collective-permute-done.7.refs_5_), channel_id=1, source_target_pairs={{0,96},{8,104},{16,112},{24,120},{32,0},{40,8},{48,16},{56,24},{64... | collective-permute-start | bytes 1572872 | tf_op jit(solution)/shard_map/ppermute | solution.py:54
  79.8 2.4 %collective-permute-start.20 = (bf16[384,1024]{1,0:T(8,128)(2,1)S(1)}, bf16[384,1024]{1,0:T(8,128)(2,1)S(1)}, u32[]{:S(2)}, u32[]{:S(2)}) collective-permute-start(bf16[384,1024]{1,0:T(8,128)(2,1)S(1)} %get-tuple-element.34.refs_0_.refs_2_), channel_id=1, source_target_pairs={{0,1},{1,0},{2,3},{3,2},{4,5},{5,4},{6,7},{7,6},{8,9},{9,8},{10,11... | collective-permute-start | bytes 2359304 | tf_op jit(solution)/shard_map/ppermute | solution.py:369
  80.1 15.4 %copy-start = (bf16[16384,128]{1,0:T(8,128)(2,1)S(1)}, bf16[16384,128]{1,0:T(8,128)(2,1)}, u32[]{:S(2)}) copy-start(bf16[16384,128]{1,0:T(8,128)(2,1)} %get-tuple-element.38.k_all) | copy-start | bytes 12582916
  80.1 15.4 %copy-start.1 = (bf16[16384,128]{1,0:T(8,128)(2,1)S(1)}, bf16[16384,128]{1,0:T(8,128)(2,1)}, u32[]{:S(2)}) copy-start(bf16[16384,128]{1,0:T(8,128)(2,1)} %get-tuple-element.39.v_all) | copy-start | bytes 12582916
  90.8 21.9 %collective-permute-start.23 = (bf16[384,1024]{1,0:T(8,128)(2,1)S(1)}, bf16[384,1024]{1,0:T(8,128)(2,1)S(1)}, u32[]{:S(2)}, u32[]{:S(2)}) collective-permute-start(bf16[384,1024]{1,0:T(8,128)(2,1)S(1)} %get-tuple-element.42), channel_id=1, source_target_pairs={{0,6},{1,7},{2,0},{3,1},{4,2},{5,3},{6,4},{7,5},{8,14},{9,15},{10,... | collective-permute-start | bytes 2359304 | tf_op jit(solution)/shard_map/ppermute | solution.py:345
  95.5 21.0 %collective-permute-start.22 = (bf16[384,1024]{1,0:T(8,128)(2,1)S(1)}, bf16[384,1024]{1,0:T(8,128)(2,1)S(1)}, u32[]{:S(2)}, u32[]{:S(2)}) collective-permute-start(bf16[384,1024]{1,0:T(8,128)(2,1)S(1)} %get-tuple-element.40), channel_id=1, source_target_pairs={{0,2},{1,3},{2,4},{3,5},{4,6},{5,7},{6,0},{7,1},{8,10},{9,11},{10,... | collective-permute-start | bytes 2359304 | tf_op jit(solution)/shard_map/ppermute | solution.py:345
  103.2 13.7 %collective-permute-start.24 = (bf16[384,1024]{1,0:T(8,128)(2,1)S(1)}, bf16[384,1024]{1,0:T(8,128)(2,1)S(1)}, u32[]{:S(2)}, u32[]{:S(2)}) collective-permute-start(bf16[384,1024]{1,0:T(8,128)(2,1)S(1)} %attend.2.refs_0_.refs_2_), channel_id=1, source_target_pairs={{0,1},{1,0},{2,3},{3,2},{4,5},{5,4},{6,7},{7,6},{8,9},{9,8},{10,11... | collective-permute-start | bytes 2359304 | tf_op jit(solution)/shard_map/ppermute | solution.py:369
  112.7 17.9 %collective-permute-start.26 = (bf16[192,1024]{1,0:T(8,128)(2,1)S(1)}, bf16[192,1024]{1,0:T(8,128)(2,1)S(1)}, u32[]{:S(2)}, u32[]{:S(2)}) collective-permute-start(bf16[192,1024]{1,0:T(8,128)(2,1)S(1)} %add_convert_fusion.6), channel_id=1, source_target_pairs={{0,6},{1,7},{2,0},{3,1},{4,2},{5,3},{6,4},{7,5},{8,14},{9,15},{10,... | collective-permute-start | bytes 1179656 | tf_op jit(solution)/shard_map/ppermute | solution.py:345
  116.6 14.1 %collective-permute-start.25 = (bf16[192,1024]{1,0:T(8,128)(2,1)S(1)}, bf16[192,1024]{1,0:T(8,128)(2,1)S(1)}, u32[]{:S(2)}, u32[]{:S(2)}) collective-permute-start(bf16[192,1024]{1,0:T(8,128)(2,1)S(1)} %add_convert_fusion.7), channel_id=1, source_target_pairs={{0,2},{1,3},{2,4},{3,5},{4,6},{5,7},{6,0},{7,1},{8,10},{9,11},{10,... | collective-permute-start | bytes 1179656 | tf_op jit(solution)/shard_map/ppermute | solution.py:345
  127.4 22.7 %collective-permute-start.28 = (bf16[384,1024]{1,0:T(8,128)(2,1)S(1)}, bf16[384,1024]{1,0:T(8,128)(2,1)S(1)}, u32[]{:S(2)}, u32[]{:S(2)}) collective-permute-start(bf16[384,1024]{1,0:T(8,128)(2,1)S(1)} %get-tuple-element.50), channel_id=1, source_target_pairs={{0,6},{1,7},{2,0},{3,1},{4,2},{5,3},{6,4},{7,5},{8,14},{9,15},{10,... | collective-permute-start | bytes 2359304 | tf_op jit(solution)/shard_map/ppermute | solution.py:345
  130.7 19.2 %collective-permute-start.27 = (bf16[384,1024]{1,0:T(8,128)(2,1)S(1)}, bf16[384,1024]{1,0:T(8,128)(2,1)S(1)}, u32[]{:S(2)}, u32[]{:S(2)}) collective-permute-start(bf16[384,1024]{1,0:T(8,128)(2,1)S(1)} %get-tuple-element.48), channel_id=1, source_target_pairs={{0,2},{1,3},{2,4},{3,5},{4,6},{5,7},{6,0},{7,1},{8,10},{9,11},{10,... | collective-permute-start | bytes 2359304 | tf_op jit(solution)/shard_map/ppermute | solution.py:345
  136.5 16.9 %collective-permute-start.29 = (bf16[256,1024]{1,0:T(8,128)(2,1)S(1)}, bf16[256,1024]{1,0:T(8,128)(2,1)S(1)}, u32[]{:S(2)}, u32[]{:S(2)}) collective-permute-start(bf16[256,1024]{1,0:T(8,128)(2,1)S(1)} %attend.3.refs_0_), channel_id=1, source_target_pairs={{0,1},{1,0},{2,3},{3,2},{4,5},{5,4},{6,7},{7,6},{8,9},{9,8},{10,11... | collective-permute-start | bytes 1572872 | tf_op jit(solution)/shard_map/ppermute | solution.py:369
  150.0 18.4 %collective-permute-start.30 = (bf16[192,1024]{1,0:T(8,128)(2,1)S(1)}, bf16[192,1024]{1,0:T(8,128)(2,1)S(1)}, u32[]{:S(2)}, u32[]{:S(2)}) collective-permute-start(bf16[192,1024]{1,0:T(8,128)(2,1)S(1)} %add_convert_fusion.3), channel_id=1, source_target_pairs={{0,2},{1,3},{2,4},{3,5},{4,6},{5,7},{6,0},{7,1},{8,10},{9,11},{10,... | collective-permute-start | bytes 1179656 | tf_op jit(solution)/shard_map/ppermute | solution.py:345
  150.2 26.3 %collective-permute-start.31 = (bf16[192,1024]{1,0:T(8,128)(2,1)S(1)}, bf16[192,1024]{1,0:T(8,128)(2,1)S(1)}, u32[]{:S(2)}, u32[]{:S(2)}) collective-permute-start(bf16[192,1024]{1,0:T(8,128)(2,1)S(1)} %add_convert_fusion.2), channel_id=1, source_target_pairs={{0,6},{1,7},{2,0},{3,1},{4,2},{5,3},{6,4},{7,5},{8,14},{9,15},{10,... | collective-permute-start | bytes 1179656 | tf_op jit(solution)/shard_map/ppermute | solution.py:345
  162.2 12.0 %collective-permute-start.34 = (bf16[256,1024]{1,0:T(8,128)(2,1)S(1)}, bf16[256,1024]{1,0:T(8,128)(2,1)S(1)}, u32[]{:S(2)}, u32[]{:S(2)}) collective-permute-start(bf16[256,1024]{1,0:T(8,128)(2,1)S(1)} %get-tuple-element.55), channel_id=1, source_target_pairs={{0,6},{1,7},{2,0},{3,1},{4,2},{5,3},{6,4},{7,5},{8,14},{9,15},{10,... | collective-permute-start | bytes 1572872 | tf_op jit(solution)/shard_map/ppermute | solution.py:345
  162.3 12.5 %collective-permute-start.32 = (bf16[256,1024]{1,0:T(8,128)(2,1)S(1)}, bf16[256,1024]{1,0:T(8,128)(2,1)S(1)}, u32[]{:S(2)}, u32[]{:S(2)}) collective-permute-start(bf16[256,1024]{1,0:T(8,128)(2,1)S(1)} %get-tuple-element.54), channel_id=1, source_target_pairs={{0,2},{1,3},{2,4},{3,5},{4,6},{5,7},{6,0},{7,1},{8,10},{9,11},{10,... | collective-permute-start | bytes 1572872 | tf_op jit(solution)/shard_map/ppermute | solution.py:345
  174.3 8.3 %collective-permute-start.35 = (bf16[128,1024]{1,0:T(8,128)(2,1)S(1)}, bf16[128,1024]{1,0:T(8,128)(2,1)S(1)}, u32[]{:S(2)}, u32[]{:S(2)}) collective-permute-start(bf16[128,1024]{1,0:T(8,128)(2,1)S(1)} %add_convert_fusion.8), channel_id=1, source_target_pairs={{0,6},{1,7},{2,0},{3,1},{4,2},{5,3},{6,4},{7,5},{8,14},{9,15},{10,... | collective-permute-start | bytes 786440 | tf_op jit(solution)/shard_map/ppermute | solution.py:345
  174.8 7.7 %collective-permute-start.33 = (bf16[128,1024]{1,0:T(8,128)(2,1)S(1)}, bf16[128,1024]{1,0:T(8,128)(2,1)S(1)}, u32[]{:S(2)}, u32[]{:S(2)}) collective-permute-start(bf16[128,1024]{1,0:T(8,128)(2,1)S(1)} %add_convert_fusion.9), channel_id=1, source_target_pairs={{0,2},{1,3},{2,4},{3,5},{4,6},{5,7},{6,0},{7,1},{8,10},{9,11},{10,... | collective-permute-start | bytes 786440 | tf_op jit(solution)/shard_map/ppermute | solution.py:345
  182.6 1.3 copy-start.6
  (1 other events, 0.8 us)
where the time goes:
time: 185 us
  waiting for transfers between devices  68.1 us (37%)
  Pallas kernels  55.8 us (30%)
  starting transfers between devices  43.5 us (24%)
  local copies, waits for them, and re-layouts  11.6 us (6%)
  other arithmetic  5.17 us (3%)
    ppermute x12, waiting for transfers between devices, send(): return lax.ppermute(piece, 'tensor', along_y(step))  32.3 us
    ppermute x12, waiting for transfers between devices, pass_on(): return lax.ppermute(part, 'seq', second(step))  32.2 us
    pallas_call x4, Pallas kernels, product(): pl.pallas_call(functools.partial(product_kernel, sends, owns), out_shape=...  31.8 us
    ppermute x12, starting transfers between devices, send(): return lax.ppermute(piece, 'tensor', along_y(step))  19.7 us
    pallas_call x2, Pallas kernels, attend(): pl.pallas_call(functools.partial(attend_kernel, kmax), out_shape=out, in_...  13.5 us
    ppermute x12, starting transfers between devices, pass_on(): return lax.ppermute(part, 'seq', second(step))  12.4 us
    pallas_call x1, Pallas kernels, attend(): pl.pallas_call(functools.partial(attend_first_kernel, kmax), out_shape=[o...  10.5 us
    unnamed x32, local copies, waits for them, and re-layouts  6.68 us
  transfers between devices with their start and end apart: 36, of which 15 were waited for; matrix products, arithmetic and copies ran while one was open for 7% of the time, Pallas kernels for 26%

commit v1 on v0

--- a/solution.py
+++ b/solution.py
@@ -13,7 +13,7 @@
 SIDE = 4
 CORES = 2
 PARTS = 8
-CHUNKS = (3, 3, 2)
+CHUNKS = (4, 4)
 VARIANTS = (1, 2, 3, 4, 6, 8)
 ORDER = (2, 1, 3, 0)
 COST = 2
@@ -339,7 +339,7 @@
     plans = tables(key_blocks, block_counts, seq_index, tokens // BLOCK)
 
     cols = jnp.stack([(y + step) % SIDE * CORES + core for step in ORDER]).astype(jnp.int32)
-    theirs = lax.ppermute(after(out_weight, *k_parts[:2], *v_parts[:2]), "tensor", other_core())
+    theirs = lax.ppermute(out_weight, "tensor", other_core())
 
     def send(piece, step):
         return lax.ppermute(piece, "tensor", along_y(step))

time: 185 us -> 178 us (0.962)
  starting transfers between devices: 43.5 us -> 35.6 us
  waiting for transfers between devices: 68.1 us -> 74 us
  local copies, waits for them, and re-layouts: 11.6 us -> 6.04 us
  other arithmetic: 5.17 us -> 8.51 us
  Pallas kernels: 55.8 us -> 52.5 us
    ppermute x12 -> x8, waiting for transfers between devices: 32.3 us -> 44.7 us  [send(): return lax.ppermute(piece, 'tensor', along_y(step))]
    ppermute x12, waiting for transfers between devices: 32.2 us -> 24 us  [pass_on(): return lax.ppermute(part, 'seq', second(step))]
    ppermute x12 -> x8, starting transfers between devices: 19.7 us -> 14.6 us  [send(): return lax.ppermute(piece, 'tensor', along_y(step))]
    pallas_call x4 -> x3, Pallas kernels: 31.8 us -> 28.1 us  [product(): pl.pallas_call(functools.partial(product_kernel, sends, owns), out_shape=...]
    unnamed x32 -> x22, local copies, waits for them, and re-layouts: 6.68 us -> 3.37 us
    pallas_call x1, Pallas kernels: 10.5 us -> 13.5 us  [attend(): pl.pallas_call(functools.partial(attend_first_kernel, kmax), out_shape=[o...]
    ppermute x2, waiting for transfers between devices: 0.01 us -> 2.77 us  [ring(): far_high = lax.ppermute(after[half:], 'seq', perm(-1))]
    pallas_call x2 -> x1, Pallas kernels: 13.5 us -> 10.8 us  [attend(): pl.pallas_call(functools.partial(attend_kernel, kmax), out_shape=out, in_...]
  transfers between devices with their start and end apart: 36 -> 31, of which waited for: 15 -> 16; matrix products, arithmetic and copies ran while one was open for 7% -> 7% of each run, Pallas kernels for 26% -> 17%
where the time goes in v1:
time: 178 us; the launch traced here: 177 us
  waiting for transfers between devices  74 us (42%)
  Pallas kernels  52.5 us (29%)
  starting transfers between devices  35.6 us (20%)
  other arithmetic  8.51 us (5%)
  local copies, waits for them, and re-layouts  6.04 us (3%)
    ppermute x8, waiting for transfers between devices, send(): return lax.ppermute(piece, 'tensor', along_y(step))  44.7 us
    pallas_call x3, Pallas kernels, product(): pl.pallas_call(functools.partial(product_kernel, sends, owns), out_shape=...  28.1 us
    ppermute x12, waiting for transfers between devices, pass_on(): return lax.ppermute(part, 'seq', second(step))  24 us
    ppermute x8, starting transfers between devices, send(): return lax.ppermute(piece, 'tensor', along_y(step))  14.6 us
    pallas_call x1, Pallas kernels, attend(): pl.pallas_call(functools.partial(attend_first_kernel, kmax), out_shape=[o...  13.5 us
    pallas_call x1, Pallas kernels, attend(): pl.pallas_call(functools.partial(attend_kernel, kmax), out_shape=out, in_...  10.8 us
    ppermute x12, starting transfers between devices, pass_on(): return lax.ppermute(part, 'seq', second(step))  9.75 us
    ppermute x2, starting transfers between devices, ring(): far_high = lax.ppermute(after[half:], 'seq', perm(-1))  3.91 us
  transfers between devices with their start and end apart: 31, of which 16 were waited for; matrix products, arithmetic and copies ran while one was open for 7% of the time, Pallas kernels for 17%

profile of v1, /device:TPU:96, one launch (start us, length us, event | category | flops | bytes accessed | tf_op | source)
XLA Modules:
  0.0 177.0 jit_solution(8818917788716477379)
XLA Ops:
  0.0 1.5 collective-permute-start
  1.5 1.7 collective-permute-start.1
  3.2 2.0 %collective-permute-start.11 = (bf16[1024,128]{1,0:T(8,128)(2,1)}, bf16[1024,128]{1,0:T(8,128)(2,1)S(1)}, u32[]{:S(2)}, u32[]{:S(2)}) collective-permute-start(bf16[1024,128]{1,0:T(8,128)(2,1)} %param.9), channel_id=1, source_target_pairs={{0,96},{8,104},{16,112},{24,120},{32,0},{40,8},{48,16},{56,24},{64... | collective-permute-start | bytes 786440 | tf_op jit(solution)/shard_map/ppermute | solution.py:42
  5.3 1.0 constant_dynamic-update-slice_fusion.1
  6.2 1.0 constant_dynamic-update-slice_fusion.6
  7.2 0.8 fusion.11
  8.0 1.1 add_bitcast_fusion
  9.1 1.1 add_bitcast_fusion.1
  10.6 3.0 %collective-permute-start.3 = (bf16[512,128]{1,0:T(8,128)(2,1)S(1)}, bf16[512,128]{1,0:T(8,128)(2,1)S(1)}, u32[]{:S(2)}, u32[]{:S(2)}) collective-permute-start(bf16[512,128]{1,0:T(8,128)(2,1)S(1)} %slice.133), channel_id=1, source_target_pairs={{0,24},{8,0},{16,8},{24,16},{32,56},{40,32},{48,40},{56,48},{64,88... | collective-permute-start | bytes 393224 | tf_op jit(solution)/shard_map/ppermute | solution.py:44
  13.7 1.3 collective-permute-start.12
  15.0 0.9 collective-permute-start.13
  15.9 0.7 constant_dynamic-update-slice_fusion.4
  17.1 1.7 collective-permute-start.14
  19.2 2.8 %collective-permute-done.13 = bf16[512,128]{1,0:T(8,128)(2,1)S(1)} collective-permute-done((bf16[512,128]{1,0:T(8,128)(2,1)S(1)}, bf16[512,128]{1,0:T(8,128)(2,1)S(1)}, u32[]{:S(2)}, u32[]{:S(2)}) %collective-permute-start.13) | collective-permute-done | bytes 131104 | tf_op jit(solution)/shard_map/ppermute | solution.py:44
  22.1 0.7 constant_dynamic-update-slice_fusion.3
  22.7 0.7 constant_dynamic-update-slice_fusion.2.refs_1_
  23.4 5.6 %collective-permute-done.16.refs_12_ = bf16[2048,128]{1,0:T(8,128)(2,1)S(1)} collective-permute-done((bf16[2048,128]{1,0:T(8,128)(2,1)S(1)}, bf16[2048,128]{1,0:T(8,128)(2,1)S(1)}, u32[]{:S(2)}, u32[]{:S(2)}) %collective-permute-start.16) | collective-permute-done | bytes 524320 | tf_op jit(solution)/shard_map/ppermute | solution.py:54
  29.1 2.0 %collective-permute-start.17 = (bf16[2048,128]{1,0:T(8,128)(2,1)S(1)}, bf16[2048,128]{1,0:T(8,128)(2,1)}, u32[]{:S(2)}, u32[]{:S(2)}) collective-permute-start(bf16[2048,128]{1,0:T(8,128)(2,1)S(1)} %constant_dynamic-update-slice_fusion.7.refs_9_), channel_id=1, source_target_pairs={{0,24},{8,0},{16,8},{24,16},{32,56},{40,32},{48,40},{56,48},{64,88... | collective-permute-start | bytes 1572872 | tf_op jit(solution)/shard_map/ppermute | solution.py:54
  31.1 1.3 collective-permute-done.6.refs_4_
  32.8 2.9 %collective-permute-start.5 = (bf16[2048,128]{1,0:T(8,128)(2,1)}, bf16[2048,128]{1,0:T(8,128)(2,1)}, u32[]{:S(2)}, u32[]{:S(2)}) collective-permute-start(bf16[2048,128]{1,0:T(8,128)(2,1)} %constant_dynamic-update-slice_fusion.2.refs_1_), channel_id=1, source_target_pairs={{0,32},{8,40},{16,48},{24,56},{32,64},{40,72},{48,80},{56,88},{64,... | collective-permute-start | bytes 1572872 | tf_op jit(solution)/shard_map/ppermute | solution.py:54
  37.3 2.1 %sort.17 = (s32[64]{0:T(128)}, s32[64]{0:T(128)S(1)}) sort(s32[64]{0:T(128)S(1)} %reshape.13, s32[64]{0:T(128)S(1)} %iota.4), dimensions={0}, to_apply=%region_0.1 | sort | flops 384 | bytes 1024 | tf_op jit(solution)/shard_map/jit(argsort)/sort | solution.py:221
  39.4 1.3 collective-permute-done.17.refs_13_
  40.7 4.7 %collective-permute-done.15.refs_11_ = bf16[2048,128]{1,0:T(8,128)(2,1)} collective-permute-done((bf16[2048,128]{1,0:T(8,128)(2,1)S(1)}, bf16[2048,128]{1,0:T(8,128)(2,1)}, u32[]{:S(2)}, u32[]{:S(2)}) %collective-permute-start.15) | collective-permute-done | bytes 524320 | tf_op jit(solution)/shard_map/ppermute | solution.py:54
  45.4 1.9 %collective-permute-start.8 = (bf16[2048,128]{1,0:T(8,128)(2,1)}, bf16[2048,128]{1,0:T(8,128)(2,1)}, u32[]{:S(2)}, u32[]{:S(2)}) collective-permute-start(bf16[2048,128]{1,0:T(8,128)(2,1)} %collective-permute-done.4.refs_2_), channel_id=1, source_target_pairs={{0,32},{8,40},{16,48},{24,56},{32,64},{40,72},{48,80},{56,88},{64,... | collective-permute-start | bytes 1572872 | tf_op jit(solution)/shard_map/ppermute | solution.py:54
  48.1 7.1 %collective-permute-done.18.refs_14_ = bf16[2048,128]{1,0:T(8,128)(2,1)} collective-permute-done((bf16[2048,128]{1,0:T(8,128)(2,1)}, bf16[2048,128]{1,0:T(8,128)(2,1)}, u32[]{:S(2)}, u32[]{:S(2)}) %collective-permute-start.18) | collective-permute-done | bytes 524320 | tf_op jit(solution)/shard_map/ppermute | solution.py:54
  55.2 1.0 collective-permute-done.8.refs_6_
  56.1 0.6 collective-permute-done.19.refs_15_
  56.7 2.0 %collective-permute-done.9.refs_7_ = bf16[2048,128]{1,0:T(8,128)(2,1)} collective-permute-done((bf16[2048,128]{1,0:T(8,128)(2,1)}, bf16[2048,128]{1,0:T(8,128)(2,1)}, u32[]{:S(2)}, u32[]{:S(2)}) %collective-permute-start.9) | collective-permute-done | bytes 524320 | tf_op jit(solution)/shard_map/ppermute | solution.py:54
  58.7 13.5 %attend_first.1 = (bf16[512,1024]{1,0:T(8,128)(2,1)S(1)}, bf16[16384,128]{1,0:T(8,128)(2,1)}, bf16[16384,128]{1,0:T(8,128)(2,1)}) custom-call(s32[1088]{0:T(1024)S(1)} %concatenate.21.tab, bf16[512,1024]{1,0:T(8,128)(2,1)S(1)} %get-tuple-element.48.q_ref, bf16[2048,128]{1,0:T(8,128)(2,1)} %copy-done.4, ...), custom_call_target="tpu_custom_call" | custom-call | flops 8589934592 | bytes 5242880 | tf_op jit(solution)/shard_map/attend_first/pallas_call | solution.py:181
  72.5 2.5 %collective-permute-done.20.refs_1_.refs_3_ = bf16[512,1024]{1,0:T(8,128)(2,1)S(1)} collective-permute-done((bf16[512,1024]{1,0:T(8,128)(2,1)S(1)}, bf16[512,1024]{1,0:T(8,128)(2,1)S(1)}, u32[]{:S(2)}, u32[]{:S(2)}) %collective-permute-start.20) | collective-permute-done | bytes 1048608 | tf_op jit(solution)/shard_map/ppermute | solution.py:369
  75.0 10.3 %product.3 = (bf16[512,1024]{1,0:T(8,128)(2,1)S(1)}, bf16[512,1024]{1,0:T(8,128)(2,1)S(1)}, f32[256,1024]{1,0:T(8,128)S(1)}, f32[256,1024]{1,0:T(8,128)S(1)}) custom-call(s32[4]{0:T(128)S(1)} %pad_add_fusion.cols, bf16[512,1024]{1,0:T(8,128)(2,1)S(1)} %get-tuple-element.25.refs_0_.refs_2_, bf16[512,1024]{1,0:T(8,128)(2,1)S(1)} %collective-permute-done.20.refs_1_.refs_3_, ...), custom_call_target="tpu_custom_call" | custom-call | flops 25769803776 | bytes 8388608 | tf_op jit(solution)/shard_map/product/pallas_call | solution.py:304
  85.3 4.0 %collective-permute-start.22 = (bf16[512,1024]{1,0:T(8,128)(2,1)S(1)}, bf16[512,1024]{1,0:T(8,128)(2,1)S(1)}, u32[]{:S(2)}, u32[]{:S(2)}) collective-permute-start(bf16[512,1024]{1,0:T(8,128)(2,1)S(1)} %get-tuple-element.30), channel_id=1, source_target_pairs={{0,2},{1,3},{2,4},{3,5},{4,6},{5,7},{6,0},{7,1},{8,10},{9,11},{10,... | collective-permute-start | bytes 3145736 | tf_op jit(solution)/shard_map/ppermute | solution.py:345
  89.3 0.7 collective-permute-start.23
  90.0 10.8 %attend.1.refs_0_ = bf16[512,1024]{1,0:T(8,128)(2,1)S(1)} custom-call(s32[1088]{0:T(1024)S(1)} %concatenate.22.tab, bf16[512,1024]{1,0:T(8,128)(2,1)S(1)} %get-tuple-element.47.q_ref, bf16[16384,128]{1,0:T(8,128)(2,1)S(1)} %copy-done, bf16[16384,128]{1,0:T(8,128)(2,1)S(1)} %copy-done.1), custom_call_target="tpu_custom_call" | custom-call | flops 8589934592 | bytes 5242880 | tf_op jit(solution)/shard_map/attend/pallas_call | solution.py:191
  101.2 12.2 %collective-permute-done.22 = bf16[512,1024]{1,0:T(8,128)(2,1)S(1)} collective-permute-done((bf16[512,1024]{1,0:T(8,128)(2,1)S(1)}, bf16[512,1024]{1,0:T(8,128)(2,1)S(1)}, u32[]{:S(2)}, u32[]{:S(2)}) %collective-permute-start.22) | collective-permute-done | bytes 1048608 | tf_op jit(solution)/shard_map/ppermute | solution.py:345
  113.6 0.7 collective-permute-done.23
  114.4 12.7 %product.4 = (bf16[512,1024]{1,0:T(8,128)(2,1)S(1)}, bf16[512,1024]{1,0:T(8,128)(2,1)S(1)}, f32[256,1024]{1,0:T(8,128)S(1)}, f32[256,1024]{1,0:T(8,128)S(1)}, f32[512,1024]{1,0:T(8,128)S(1)}) custom-call(s32[4]{0:T(128)S(1)} %pad_add_fusion.cols, bf16[512,1024]{1,0:T(8,128)(2,1)S(1)} %attend.1.refs_0_, ...), custom_call_target="tpu_custom_call" | custom-call | flops 34359738368 | bytes 10485760 | tf_op jit(solution)/shard_map/product/pallas_call | solution.py:304
  127.1 0.5 collective-permute-start.27
  127.6 2.8 %collective-permute-start.29 = (bf16[512,1024]{1,0:T(8,128)(2,1)S(1)}, bf16[512,1024]{1,0:T(8,128)(2,1)S(1)}, u32[]{:S(2)}, u32[]{:S(2)}) collective-permute-start(bf16[512,1024]{1,0:T(8,128)(2,1)S(1)} %get-tuple-element.37), channel_id=1, source_target_pairs={{0,6},{1,7},{2,0},{3,1},{4,2},{5,3},{6,4},{7,5},{8,14},{9,15},{10,... | collective-permute-start | bytes 3145736 | tf_op jit(solution)/shard_map/ppermute | solution.py:345
  130.4 3.2 %collective-permute-start.26 = (bf16[256,1024]{1,0:T(8,128)(2,1)S(1)}, bf16[256,1024]{1,0:T(8,128)(2,1)S(1)}, u32[]{:S(2)}, u32[]{:S(2)}) collective-permute-start(bf16[256,1024]{1,0:T(8,128)(2,1)S(1)} %add_convert_fusion.4), channel_id=1, source_target_pairs={{0,6},{1,7},{2,0},{3,1},{4,2},{5,3},{6,4},{7,5},{8,14},{9,15},{10,... | collective-permute-start | bytes 1572872 | tf_op jit(solution)/shard_map/ppermute | solution.py:345
  133.7 20.8 %collective-permute-done.27 = bf16[512,1024]{1,0:T(8,128)(2,1)S(1)} collective-permute-done((bf16[512,1024]{1,0:T(8,128)(2,1)S(1)}, bf16[512,1024]{1,0:T(8,128)(2,1)S(1)}, u32[]{:S(2)}, u32[]{:S(2)}) %collective-permute-start.27) | collective-permute-done | bytes 1048608 | tf_op jit(solution)/shard_map/ppermute | solution.py:345
  154.9 3.3 %collective-permute-start.30 = (bf16[256,1024]{1,0:T(8,128)(2,1)S(1)}, bf16[256,1024]{1,0:T(8,128)(2,1)S(1)}, u32[]{:S(2)}, u32[]{:S(2)}) collective-permute-start(bf16[256,1024]{1,0:T(8,128)(2,1)S(1)} %add_convert_fusion), channel_id=1, source_target_pairs={{0,6},{1,7},{2,0},{3,1},{4,2},{5,3},{6,4},{7,5},{8,14},{9,15},{10,... | collective-permute-start | bytes 1572872 | tf_op jit(solution)/shard_map/ppermute | solution.py:345
  158.2 5.1 %product.5 = f32[512,1024]{1,0:T(8,128)S(1)} custom-call(s32[4]{0:T(128)S(1)} %pad_add_fusion.cols, bf16[512,1024]{1,0:T(8,128)(2,1)S(1)} %attend.1.refs_0_, bf16[512,1024]{1,0:T(8,128)(2,1)S(1)} %collective-permute-done.24.refs_1_, bf16[1024,8192]{1,0:T(8,128)(2,1)} %refs_2_.3, bf16[1024,8192]{1,0:T(8,128)(2,1)} %collective-permute-done.21.refs_3_.refs_5_), custom_call_target="tpu_custom_call" | custom-call | flops 8589934592 | bytes 4194304 | tf_op jit(solution)/shard_map/product/pallas_call | solution.py:304
  163.3 2.4 %collective-permute-done.25 = bf16[256,1024]{1,0:T(8,128)(2,1)S(1)} collective-permute-done((bf16[256,1024]{1,0:T(8,128)(2,1)S(1)}, bf16[256,1024]{1,0:T(8,128)(2,1)S(1)}, u32[]{:S(2)}, u32[]{:S(2)}) %collective-permute-start.25) | collective-permute-done | bytes 524320 | tf_op jit(solution)/shard_map/ppermute | solution.py:345
  165.7 0.6 add_convert_fusion.3
  166.3 8.6 %collective-permute-done.28 = bf16[256,1024]{1,0:T(8,128)(2,1)S(1)} collective-permute-done((bf16[256,1024]{1,0:T(8,128)(2,1)S(1)}, bf16[256,1024]{1,0:T(8,128)(2,1)S(1)}, u32[]{:S(2)}, u32[]{:S(2)}) %collective-permute-start.28) | collective-permute-done | bytes 524320 | tf_op jit(solution)/shard_map/ppermute | solution.py:345
  174.9 0.6 fusion.3
  175.5 1.5 pad_maximum_fusion
  (83 shorter events, 5.5 us)
Async XLA Ops:
  0.0 75.0 %collective-permute-start.21 = (bf16[1024,8192]{1,0:T(8,128)(2,1)}, bf16[1024,8192]{1,0:T(8,128)(2,1)}, u32[]{:S(2)}, u32[]{:S(2)}) collective-permute-start(bf16[1024,8192]{1,0:T(8,128)(2,1)} %refs_2_.3), channel_id=1, source_target_pairs={{0,1},{1,0},{2,3},{3,2},{4,5},{5,4},{6,7},{7,6},{8,9},{9,8},{10,11... | collective-permute-start | bytes 50331656 | tf_op jit(solution)/shard_map/ppermute | solution.py:342
  0.0 10.2 %collective-permute-start = (bf16[1024,128]{1,0:T(8,128)(2,1)}, bf16[1024,128]{1,0:T(8,128)(2,1)S(1)}, u32[]{:S(2)}, u32[]{:S(2)}) collective-permute-start(bf16[1024,128]{1,0:T(8,128)(2,1)} %param.8), channel_id=1, source_target_pairs={{0,8},{8,16},{16,24},{24,0},{32,40},{40,48},{48,56},{56,32},{64,72... | collective-permute-start | bytes 786440 | tf_op jit(solution)/shard_map/ppermute | solution.py:41
  1.5 9.1 %collective-permute-start.1 = (bf16[1024,128]{1,0:T(8,128)(2,1)}, bf16[1024,128]{1,0:T(8,128)(2,1)S(1)}, u32[]{:S(2)}, u32[]{:S(2)}) collective-permute-start(bf16[1024,128]{1,0:T(8,128)(2,1)} %param.8), channel_id=1, source_target_pairs={{0,24},{8,0},{16,8},{24,16},{32,56},{40,32},{48,40},{56,48},{64,88... | collective-permute-start | bytes 786440 | tf_op jit(solution)/shard_map/ppermute | solution.py:42
  3.2 10.4 %collective-permute-start.10 = (bf16[1024,128]{1,0:T(8,128)(2,1)}, bf16[1024,128]{1,0:T(8,128)(2,1)S(1)}, u32[]{:S(2)}, u32[]{:S(2)}) collective-permute-start(bf16[1024,128]{1,0:T(8,128)(2,1)} %param.9), channel_id=1, source_target_pairs={{0,32},{8,40},{16,48},{24,56},{32,64},{40,72},{48,80},{56,88},{64,... | collective-permute-start | bytes 786440 | tf_op jit(solution)/shard_map/ppermute | solution.py:41
  3.2 11.7 %collective-permute-start.11 = (bf16[1024,128]{1,0:T(8,128)(2,1)}, bf16[1024,128]{1,0:T(8,128)(2,1)S(1)}, u32[]{:S(2)}, u32[]{:S(2)}) collective-permute-start(bf16[1024,128]{1,0:T(8,128)(2,1)} %param.9), channel_id=1, source_target_pairs={{0,96},{8,104},{16,112},{24,120},{32,0},{40,8},{48,16},{56,24},{64... | collective-permute-start | bytes 786440 | tf_op jit(solution)/shard_map/ppermute | solution.py:42
  10.3 6.4 %collective-permute-start.2 = (bf16[512,128]{1,0:T(8,128)(2,1)S(1)}, bf16[512,128]{1,0:T(8,128)(2,1)S(1)}, u32[]{:S(2)}, u32[]{:S(2)}) collective-permute-start(bf16[512,128]{1,0:T(8,128)(2,1)S(1)} %slice.132), channel_id=1, source_target_pairs={{0,8},{8,16},{16,24},{24,0},{32,40},{40,48},{48,56},{56,32},{64,72... | collective-permute-start | bytes 393224 | tf_op jit(solution)/shard_map/ppermute | solution.py:43
  10.6 6.5 %collective-permute-start.3 = (bf16[512,128]{1,0:T(8,128)(2,1)S(1)}, bf16[512,128]{1,0:T(8,128)(2,1)S(1)}, u32[]{:S(2)}, u32[]{:S(2)}) collective-permute-start(bf16[512,128]{1,0:T(8,128)(2,1)S(1)} %slice.133), channel_id=1, source_target_pairs={{0,24},{8,0},{16,8},{24,16},{32,56},{40,32},{48,40},{56,48},{64,88... | collective-permute-start | bytes 393224 | tf_op jit(solution)/shard_map/ppermute | solution.py:44
  13.7 5.1 %collective-permute-start.12 = (bf16[512,128]{1,0:T(8,128)(2,1)S(1)}, bf16[512,128]{1,0:T(8,128)(2,1)S(1)}, u32[]{:S(2)}, u32[]{:S(2)}) collective-permute-start(bf16[512,128]{1,0:T(8,128)(2,1)S(1)} %slice.134), channel_id=1, source_target_pairs={{0,32},{8,40},{16,48},{24,56},{32,64},{40,72},{48,80},{56,88},{64,... | collective-permute-start | bytes 393224 | tf_op jit(solution)/shard_map/ppermute | solution.py:43
  15.0 32.9 %copy-start.2 = (bf16[1024,1024]{1,0:T(8,128)(2,1)S(1)}, bf16[1024,1024]{1,0:T(8,128)(2,1)}, u32[]{:S(2)}) copy-start(bf16[1024,1024]{1,0:T(8,128)(2,1)} %param.7) | copy-start | bytes 6291460
  15.0 7.0 %collective-permute-start.13 = (bf16[512,128]{1,0:T(8,128)(2,1)S(1)}, bf16[512,128]{1,0:T(8,128)(2,1)S(1)}, u32[]{:S(2)}, u32[]{:S(2)}) collective-permute-start(bf16[512,128]{1,0:T(8,128)(2,1)S(1)} %slice.135), channel_id=1, source_target_pairs={{0,96},{8,104},{16,112},{24,120},{32,0},{40,8},{48,16},{56,24},{64... | collective-permute-start | bytes 393224 | tf_op jit(solution)/shard_map/ppermute | solution.py:44
  16.6 14.5 %copy-start.4 = (bf16[2048,128]{1,0:T(8,128)(2,1)}, bf16[2048,128]{1,0:T(8,128)(2,1)S(1)}, u32[]{:S(2)}) copy-start(bf16[2048,128]{1,0:T(8,128)(2,1)S(1)} %constant_dynamic-update-slice_fusion.refs_0_) | copy-start | bytes 1572868
  16.7 5.4 %copy-start.3 = (bf16[2048,128]{1,0:T(8,128)(2,1)}, bf16[2048,128]{1,0:T(8,128)(2,1)S(1)}, u32[]{:S(2)}) copy-start(bf16[2048,128]{1,0:T(8,128)(2,1)S(1)} %constant_dynamic-update-slice_fusion.5.refs_8_) | copy-start | bytes 1572868
  16.7 12.4 %collective-permute-start.16 = (bf16[2048,128]{1,0:T(8,128)(2,1)S(1)}, bf16[2048,128]{1,0:T(8,128)(2,1)S(1)}, u32[]{:S(2)}, u32[]{:S(2)}) collective-permute-start(bf16[2048,128]{1,0:T(8,128)(2,1)S(1)} %constant_dynamic-update-slice_fusion.5.refs_8_), channel_id=1, source_target_pairs={{0,24},{8,0},{16,8},{24,16},{32,56},{40,32},{48,40},{56,48},{64,88... | collective-permute-start | bytes 1572872 | tf_op jit(solution)/shard_map/ppermute | solution.py:54
  17.1 14.0 %collective-permute-start.14 = (bf16[2048,128]{1,0:T(8,128)(2,1)S(1)}, bf16[2048,128]{1,0:T(8,128)(2,1)}, u32[]{:S(2)}, u32[]{:S(2)}) collective-permute-start(bf16[2048,128]{1,0:T(8,128)(2,1)S(1)} %constant_dynamic-update-slice_fusion.5.refs_8_), channel_id=1, source_target_pairs={{0,8},{8,16},{16,24},{24,0},{32,40},{40,48},{48,56},{56,32},{64,72... | collective-permute-start | bytes 1572872 | tf_op jit(solution)/shard_map/ppermute | solution.py:54
  18.8 13.7 %collective-permute-start.6 = (bf16[2048,128]{1,0:T(8,128)(2,1)S(1)}, bf16[2048,128]{1,0:T(8,128)(2,1)S(1)}, u32[]{:S(2)}, u32[]{:S(2)}) collective-permute-start(bf16[2048,128]{1,0:T(8,128)(2,1)S(1)} %constant_dynamic-update-slice_fusion.refs_0_), channel_id=1, source_target_pairs={{0,96},{8,104},{16,112},{24,120},{32,0},{40,8},{48,16},{56,24},{64... | collective-permute-start | bytes 1572872 | tf_op jit(solution)/shard_map/ppermute | solution.py:54
  22.0 10.9 %collective-permute-start.4 = (bf16[2048,128]{1,0:T(8,128)(2,1)S(1)}, bf16[2048,128]{1,0:T(8,128)(2,1)}, u32[]{:S(2)}, u32[]{:S(2)}) collective-permute-start(bf16[2048,128]{1,0:T(8,128)(2,1)S(1)} %constant_dynamic-update-slice_fusion.refs_0_), channel_id=1, source_target_pairs={{0,32},{8,40},{16,48},{24,56},{32,64},{40,72},{48,80},{56,88},{64,... | collective-permute-start | bytes 1572872 | tf_op jit(solution)/shard_map/ppermute | solution.py:54
  23.4 24.4 %copy-start.5 = (bf16[2048,128]{1,0:T(8,128)(2,1)}, bf16[2048,128]{1,0:T(8,128)(2,1)S(1)}, u32[]{:S(2)}) copy-start(bf16[2048,128]{1,0:T(8,128)(2,1)S(1)} %constant_dynamic-update-slice_fusion.7.refs_9_) | copy-start | bytes 1572868
  29.1 6.7 %copy-start.6 = (bf16[2048,128]{1,0:T(8,128)(2,1)}, bf16[2048,128]{1,0:T(8,128)(2,1)S(1)}, u32[]{:S(2)}) copy-start(bf16[2048,128]{1,0:T(8,128)(2,1)S(1)} %collective-permute-done.16.refs_12_) | copy-start | bytes 1572868
  29.1 11.6 %collective-permute-start.17 = (bf16[2048,128]{1,0:T(8,128)(2,1)S(1)}, bf16[2048,128]{1,0:T(8,128)(2,1)}, u32[]{:S(2)}, u32[]{:S(2)}) collective-permute-start(bf16[2048,128]{1,0:T(8,128)(2,1)S(1)} %constant_dynamic-update-slice_fusion.7.refs_9_), channel_id=1, source_target_pairs={{0,24},{8,0},{16,8},{24,16},{32,56},{40,32},{48,40},{56,48},{64,88... | collective-permute-start | bytes 1572872 | tf_op jit(solution)/shard_map/ppermute | solution.py:54
  31.1 14.3 %collective-permute-start.15 = (bf16[2048,128]{1,0:T(8,128)(2,1)S(1)}, bf16[2048,128]{1,0:T(8,128)(2,1)}, u32[]{:S(2)}, u32[]{:S(2)}) collective-permute-start(bf16[2048,128]{1,0:T(8,128)(2,1)S(1)} %constant_dynamic-update-slice_fusion.7.refs_9_), channel_id=1, source_target_pairs={{0,8},{8,16},{16,24},{24,0},{32,40},{40,48},{48,56},{56,32},{64,72... | collective-permute-start | bytes 1572872 | tf_op jit(solution)/shard_map/ppermute | solution.py:54
  32.5 3.3 %copy-start.7 = (bf16[2048,128]{1,0:T(8,128)(2,1)}, bf16[2048,128]{1,0:T(8,128)(2,1)S(1)}, u32[]{:S(2)}) copy-start(bf16[2048,128]{1,0:T(8,128)(2,1)S(1)} %collective-permute-done.6.refs_4_) | copy-start | bytes 1572868
  32.5 14.7 %collective-permute-start.7 = (bf16[2048,128]{1,0:T(8,128)(2,1)}, bf16[2048,128]{1,0:T(8,128)(2,1)}, u32[]{:S(2)}, u32[]{:S(2)}) collective-permute-start(bf16[2048,128]{1,0:T(8,128)(2,1)} %constant_dynamic-update-slice_fusion.2.refs_1_), channel_id=1, source_target_pairs={{0,96},{8,104},{16,112},{24,120},{32,0},{40,8},{48,16},{56,24},{64... | collective-permute-start | bytes 1572872 | tf_op jit(solution)/shard_map/ppermute | solution.py:54
  32.8 14.4 %collective-permute-start.5 = (bf16[2048,128]{1,0:T(8,128)(2,1)}, bf16[2048,128]{1,0:T(8,128)(2,1)}, u32[]{:S(2)}, u32[]{:S(2)}) collective-permute-start(bf16[2048,128]{1,0:T(8,128)(2,1)} %constant_dynamic-update-slice_fusion.2.refs_1_), channel_id=1, source_target_pairs={{0,32},{8,40},{16,48},{24,56},{32,64},{40,72},{48,80},{56,88},{64,... | collective-permute-start | bytes 1572872 | tf_op jit(solution)/shard_map/ppermute | solution.py:54
  40.7 14.5 %collective-permute-start.18 = (bf16[2048,128]{1,0:T(8,128)(2,1)}, bf16[2048,128]{1,0:T(8,128)(2,1)}, u32[]{:S(2)}, u32[]{:S(2)}) collective-permute-start(bf16[2048,128]{1,0:T(8,128)(2,1)} %collective-permute-done.14.refs_10_), channel_id=1, source_target_pairs={{0,8},{8,16},{16,24},{24,0},{32,40},{40,48},{48,56},{56,32},{64,72... | collective-permute-start | bytes 1572872 | tf_op jit(solution)/shard_map/ppermute | solution.py:54
  45.4 10.8 %collective-permute-start.8 = (bf16[2048,128]{1,0:T(8,128)(2,1)}, bf16[2048,128]{1,0:T(8,128)(2,1)}, u32[]{:S(2)}, u32[]{:S(2)}) collective-permute-start(bf16[2048,128]{1,0:T(8,128)(2,1)} %collective-permute-done.4.refs_2_), channel_id=1, source_target_pairs={{0,32},{8,40},{16,48},{24,56},{32,64},{40,72},{48,80},{56,88},{64,... | collective-permute-start | bytes 1572872 | tf_op jit(solution)/shard_map/ppermute | solution.py:54
  47.2 9.5 %collective-permute-start.19 = (bf16[2048,128]{1,0:T(8,128)(2,1)}, bf16[2048,128]{1,0:T(8,128)(2,1)}, u32[]{:S(2)}, u32[]{:S(2)}) collective-permute-start(bf16[2048,128]{1,0:T(8,128)(2,1)} %collective-permute-done.17.refs_13_), channel_id=1, source_target_pairs={{0,24},{8,0},{16,8},{24,16},{32,56},{40,32},{48,40},{56,48},{64,88... | collective-permute-start | bytes 1572872 | tf_op jit(solution)/shard_map/ppermute | solution.py:54
  47.2 11.5 %collective-permute-start.9 = (bf16[2048,128]{1,0:T(8,128)(2,1)}, bf16[2048,128]{1,0:T(8,128)(2,1)}, u32[]{:S(2)}, u32[]{:S(2)}) collective-permute-start(bf16[2048,128]{1,0:T(8,128)(2,1)} %collective-permute-done.7.refs_5_), channel_id=1, source_target_pairs={{0,96},{8,104},{16,112},{24,120},{32,0},{40,8},{48,16},{56,24},{64... | collective-permute-start | bytes 1572872 | tf_op jit(solution)/shard_map/ppermute | solution.py:54
  72.3 2.7 %collective-permute-start.20 = (bf16[512,1024]{1,0:T(8,128)(2,1)S(1)}, bf16[512,1024]{1,0:T(8,128)(2,1)S(1)}, u32[]{:S(2)}, u32[]{:S(2)}) collective-permute-start(bf16[512,1024]{1,0:T(8,128)(2,1)S(1)} %get-tuple-element.25.refs_0_.refs_2_), channel_id=1, source_target_pairs={{0,1},{1,0},{2,3},{3,2},{4,5},{5,4},{6,7},{7,6},{8,9},{9,8},{10,11... | collective-permute-start | bytes 3145736 | tf_op jit(solution)/shard_map/ppermute | solution.py:369
  72.5 17.5 %copy-start = (bf16[16384,128]{1,0:T(8,128)(2,1)S(1)}, bf16[16384,128]{1,0:T(8,128)(2,1)}, u32[]{:S(2)}) copy-start(bf16[16384,128]{1,0:T(8,128)(2,1)} %get-tuple-element.28.k_all) | copy-start | bytes 12582916
  72.5 17.5 %copy-start.1 = (bf16[16384,128]{1,0:T(8,128)(2,1)S(1)}, bf16[16384,128]{1,0:T(8,128)(2,1)}, u32[]{:S(2)}) copy-start(bf16[16384,128]{1,0:T(8,128)(2,1)} %get-tuple-element.29.v_all) | copy-start | bytes 12582916
  85.3 28.1 %collective-permute-start.22 = (bf16[512,1024]{1,0:T(8,128)(2,1)S(1)}, bf16[512,1024]{1,0:T(8,128)(2,1)S(1)}, u32[]{:S(2)}, u32[]{:S(2)}) collective-permute-start(bf16[512,1024]{1,0:T(8,128)(2,1)S(1)} %get-tuple-element.30), channel_id=1, source_target_pairs={{0,2},{1,3},{2,4},{3,5},{4,6},{5,7},{6,0},{7,1},{8,10},{9,11},{10,... | collective-permute-start | bytes 3145736 | tf_op jit(solution)/shard_map/ppermute | solution.py:345
  89.3 24.9 %collective-permute-start.23 = (bf16[512,1024]{1,0:T(8,128)(2,1)S(1)}, bf16[512,1024]{1,0:T(8,128)(2,1)S(1)}, u32[]{:S(2)}, u32[]{:S(2)}) collective-permute-start(bf16[512,1024]{1,0:T(8,128)(2,1)S(1)} %get-tuple-element.32), channel_id=1, source_target_pairs={{0,6},{1,7},{2,0},{3,1},{4,2},{5,3},{6,4},{7,5},{8,14},{9,15},{10,... | collective-permute-start | bytes 3145736 | tf_op jit(solution)/shard_map/ppermute | solution.py:345
  100.9 13.5 %collective-permute-start.24 = (bf16[512,1024]{1,0:T(8,128)(2,1)S(1)}, bf16[512,1024]{1,0:T(8,128)(2,1)S(1)}, u32[]{:S(2)}, u32[]{:S(2)}) collective-permute-start(bf16[512,1024]{1,0:T(8,128)(2,1)S(1)} %attend.1.refs_0_), channel_id=1, source_target_pairs={{0,1},{1,0},{2,3},{3,2},{4,5},{5,4},{6,7},{7,6},{8,9},{9,8},{10,11... | collective-permute-start | bytes 3145736 | tf_op jit(solution)/shard_map/ppermute | solution.py:369
  127.1 27.4 %collective-permute-start.27 = (bf16[512,1024]{1,0:T(8,128)(2,1)S(1)}, bf16[512,1024]{1,0:T(8,128)(2,1)S(1)}, u32[]{:S(2)}, u32[]{:S(2)}) collective-permute-start(bf16[512,1024]{1,0:T(8,128)(2,1)S(1)} %get-tuple-element.36), channel_id=1, source_target_pairs={{0,2},{1,3},{2,4},{3,5},{4,6},{5,7},{6,0},{7,1},{8,10},{9,11},{10,... | collective-permute-start | bytes 3145736 | tf_op jit(solution)/shard_map/ppermute | solution.py:345
  127.6 27.1 %collective-permute-start.29 = (bf16[512,1024]{1,0:T(8,128)(2,1)S(1)}, bf16[512,1024]{1,0:T(8,128)(2,1)S(1)}, u32[]{:S(2)}, u32[]{:S(2)}) collective-permute-start(bf16[512,1024]{1,0:T(8,128)(2,1)S(1)} %get-tuple-element.37), channel_id=1, source_target_pairs={{0,6},{1,7},{2,0},{3,1},{4,2},{5,3},{6,4},{7,5},{8,14},{9,15},{10,... | collective-permute-start | bytes 3145736 | tf_op jit(solution)/shard_map/ppermute | solution.py:345
  130.4 35.3 %collective-permute-start.25 = (bf16[256,1024]{1,0:T(8,128)(2,1)S(1)}, bf16[256,1024]{1,0:T(8,128)(2,1)S(1)}, u32[]{:S(2)}, u32[]{:S(2)}) collective-permute-start(bf16[256,1024]{1,0:T(8,128)(2,1)S(1)} %add_convert_fusion.5), channel_id=1, source_target_pairs={{0,2},{1,3},{2,4},{3,5},{4,6},{5,7},{6,0},{7,1},{8,10},{9,11},{10,... | collective-permute-start | bytes 1572872 | tf_op jit(solution)/shard_map/ppermute | solution.py:345
  130.4 35.3 %collective-permute-start.26 = (bf16[256,1024]{1,0:T(8,128)(2,1)S(1)}, bf16[256,1024]{1,0:T(8,128)(2,1)S(1)}, u32[]{:S(2)}, u32[]{:S(2)}) collective-permute-start(bf16[256,1024]{1,0:T(8,128)(2,1)S(1)} %add_convert_fusion.4), channel_id=1, source_target_pairs={{0,6},{1,7},{2,0},{3,1},{4,2},{5,3},{6,4},{7,5},{8,14},{9,15},{10,... | collective-permute-start | bytes 1572872 | tf_op jit(solution)/shard_map/ppermute | solution.py:345
  154.7 20.3 %collective-permute-start.28 = (bf16[256,1024]{1,0:T(8,128)(2,1)S(1)}, bf16[256,1024]{1,0:T(8,128)(2,1)S(1)}, u32[]{:S(2)}, u32[]{:S(2)}) collective-permute-start(bf16[256,1024]{1,0:T(8,128)(2,1)S(1)} %add_convert_fusion.1), channel_id=1, source_target_pairs={{0,2},{1,3},{2,4},{3,5},{4,6},{5,7},{6,0},{7,1},{8,10},{9,11},{10,... | collective-permute-start | bytes 1572872 | tf_op jit(solution)/shard_map/ppermute | solution.py:345
  154.9 20.0 %collective-permute-start.30 = (bf16[256,1024]{1,0:T(8,128)(2,1)S(1)}, bf16[256,1024]{1,0:T(8,128)(2,1)S(1)}, u32[]{:S(2)}, u32[]{:S(2)}) collective-permute-start(bf16[256,1024]{1,0:T(8,128)(2,1)S(1)} %add_convert_fusion), channel_id=1, source_target_pairs={{0,6},{1,7},{2,0},{3,1},{4,2},{5,3},{6,4},{7,5},{8,14},{9,15},{10,... | collective-permute-start | bytes 1572872 | tf_op jit(solution)/shard_map/ppermute | solution.py:345

commit v2 on v1

--- a/solution.py
+++ b/solution.py
@@ -379,8 +379,9 @@
         up, down, up_rest, down_rest = made
         up, down = send(up, 1), send(down, -1)
         before = attended, swapped
+    before = after(before[0], *settled), before[1]
     (own,) = product(cols, None, before, out_weight, theirs)
-    low, high = second(up, down, up_rest, down_rest)
+    low, high = second(up, down, after(up_rest, own), after(down_rest, own))
     results += finish(own, up, down, send(low, 1), send(high, -1))
     return jnp.concatenate(results, 0)
 

time: 178 us -> 171 us (0.961)
  waiting for transfers between devices: 74 us -> 66.6 us
    ppermute x8, waiting for transfers between devices: 44.7 us -> 37.3 us  [send(): return lax.ppermute(piece, 'tensor', along_y(step))]
  transfers between devices with their start and end apart: 31 -> 31, of which waited for: 16 -> 15; matrix products, arithmetic and copies ran while one was open for 7% -> 7% of each run, Pallas kernels for 17% -> 26%
where the time goes in v2:
time: 171 us; the launch traced here: 169 us
  waiting for transfers between devices  66.6 us (39%)
  Pallas kernels  53.9 us (32%)
  starting transfers between devices  34.1 us (20%)
  other arithmetic  8.5 us (5%)
  local copies, waits for them, and re-layouts  6.04 us (4%)
    ppermute x8, waiting for transfers between devices, send(): return lax.ppermute(piece, 'tensor', along_y(step))  37.3 us
    pallas_call x3, Pallas kernels, product(): pl.pallas_call(functools.partial(product_kernel, sends, owns), out_shape=...  28.1 us
    ppermute x12, waiting for transfers between devices, pass_on(): return lax.ppermute(part, 'seq', second(step))  24 us
    pallas_call x1, Pallas kernels, attend(): pl.pallas_call(functools.partial(attend_first_kernel, kmax), out_shape=[o...  14.3 us
    ppermute x8, starting transfers between devices, send(): return lax.ppermute(piece, 'tensor', along_y(step))  13.3 us
    pallas_call x1, Pallas kernels, attend(): pl.pallas_call(functools.partial(attend_kernel, kmax), out_shape=out, in_...  11.5 us
    ppermute x12, starting transfers between devices, pass_on(): return lax.ppermute(part, 'seq', second(step))  9.75 us
    ppermute x2, starting transfers between devices, ring(): far_high = lax.ppermute(after[half:], 'seq', perm(-1))  3.91 us
  transfers between devices with their start and end apart: 31, of which 15 were waited for; matrix products, arithmetic and copies ran while one was open for 7% of the time, Pallas kernels for 26%

profile of v2, /device:TPU:96, one launch (start us, length us, event | category | flops | bytes accessed | tf_op | source)
XLA Modules:
  0.0 169.5 jit_solution(15521432519541281745)
XLA Ops:
  0.0 1.5 collective-permute-start
  1.5 1.7 %collective-permute-start.1 = (bf16[1024,128]{1,0:T(8,128)(2,1)}, bf16[1024,128]{1,0:T(8,128)(2,1)S(1)}, u32[]{:S(2)}, u32[]{:S(2)}) collective-permute-start(bf16[1024,128]{1,0:T(8,128)(2,1)} %param.8), channel_id=1, source_target_pairs={{0,24},{8,0},{16,8},{24,16},{32,56},{40,32},{48,40},{56,48},{64,88... | collective-permute-start | bytes 786440 | tf_op jit(solution)/shard_map/ppermute | solution.py:42
  3.2 2.0 %collective-permute-start.11 = (bf16[1024,128]{1,0:T(8,128)(2,1)}, bf16[1024,128]{1,0:T(8,128)(2,1)S(1)}, u32[]{:S(2)}, u32[]{:S(2)}) collective-permute-start(bf16[1024,128]{1,0:T(8,128)(2,1)} %param.9), channel_id=1, source_target_pairs={{0,96},{8,104},{16,112},{24,120},{32,0},{40,8},{48,16},{56,24},{64... | collective-permute-start | bytes 786440 | tf_op jit(solution)/shard_map/ppermute | solution.py:42
  5.3 1.0 constant_dynamic-update-slice_fusion.1
  6.2 1.0 constant_dynamic-update-slice_fusion.6
  7.2 0.8 fusion.11
  8.0 1.1 add_bitcast_fusion
  9.1 1.1 add_bitcast_fusion.1
  10.6 3.0 %collective-permute-start.3 = (bf16[512,128]{1,0:T(8,128)(2,1)S(1)}, bf16[512,128]{1,0:T(8,128)(2,1)S(1)}, u32[]{:S(2)}, u32[]{:S(2)}) collective-permute-start(bf16[512,128]{1,0:T(8,128)(2,1)S(1)} %slice.133), channel_id=1, source_target_pairs={{0,24},{8,0},{16,8},{24,16},{32,56},{40,32},{48,40},{56,48},{64,88... | collective-permute-start | bytes 393224 | tf_op jit(solution)/shard_map/ppermute | solution.py:44
  13.7 1.3 collective-permute-start.12
  15.0 0.9 collective-permute-start.13
  15.9 0.7 constant_dynamic-update-slice_fusion.4
  16.7 0.4 collective-permute-start.16
  17.1 1.7 collective-permute-start.14
  18.8 0.4 collective-permute-start.6
  19.2 2.8 %collective-permute-done.13 = bf16[512,128]{1,0:T(8,128)(2,1)S(1)} collective-permute-done((bf16[512,128]{1,0:T(8,128)(2,1)S(1)}, bf16[512,128]{1,0:T(8,128)(2,1)S(1)}, u32[]{:S(2)}, u32[]{:S(2)}) %collective-permute-start.13) | collective-permute-done | bytes 131104 | tf_op jit(solution)/shard_map/ppermute | solution.py:44
  22.1 0.7 constant_dynamic-update-slice_fusion.3
  22.7 0.7 constant_dynamic-update-slice_fusion.2.refs_1_
  23.4 5.6 %collective-permute-done.16.refs_12_ = bf16[2048,128]{1,0:T(8,128)(2,1)S(1)} collective-permute-done((bf16[2048,128]{1,0:T(8,128)(2,1)S(1)}, bf16[2048,128]{1,0:T(8,128)(2,1)S(1)}, u32[]{:S(2)}, u32[]{:S(2)}) %collective-permute-start.16) | collective-permute-done | bytes 524320 | tf_op jit(solution)/shard_map/ppermute | solution.py:54
  29.1 2.0 %collective-permute-start.17 = (bf16[2048,128]{1,0:T(8,128)(2,1)S(1)}, bf16[2048,128]{1,0:T(8,128)(2,1)}, u32[]{:S(2)}, u32[]{:S(2)}) collective-permute-start(bf16[2048,128]{1,0:T(8,128)(2,1)S(1)} %constant_dynamic-update-slice_fusion.7.refs_9_), channel_id=1, source_target_pairs={{0,24},{8,0},{16,8},{24,16},{32,56},{40,32},{48,40},{56,48},{64,88... | collective-permute-start | bytes 1572872 | tf_op jit(solution)/shard_map/ppermute | solution.py:54
  31.1 1.3 collective-permute-done.6.refs_4_
  32.8 2.9 %collective-permute-start.5 = (bf16[2048,128]{1,0:T(8,128)(2,1)}, bf16[2048,128]{1,0:T(8,128)(2,1)}, u32[]{:S(2)}, u32[]{:S(2)}) collective-permute-start(bf16[2048,128]{1,0:T(8,128)(2,1)} %constant_dynamic-update-slice_fusion.2.refs_1_), channel_id=1, source_target_pairs={{0,32},{8,40},{16,48},{24,56},{32,64},{40,72},{48,80},{56,88},{64,... | collective-permute-start | bytes 1572872 | tf_op jit(solution)/shard_map/ppermute | solution.py:54
  37.3 2.1 %sort.17 = (s32[64]{0:T(128)}, s32[64]{0:T(128)S(1)}) sort(s32[64]{0:T(128)S(1)} %reshape.13, s32[64]{0:T(128)S(1)} %iota.4), dimensions={0}, to_apply=%region_0.1 | sort | flops 384 | bytes 1024 | tf_op jit(solution)/shard_map/jit(argsort)/sort | solution.py:221
  39.4 1.3 collective-permute-done.17.refs_13_
  40.7 4.7 %collective-permute-done.15.refs_11_ = bf16[2048,128]{1,0:T(8,128)(2,1)} collective-permute-done((bf16[2048,128]{1,0:T(8,128)(2,1)S(1)}, bf16[2048,128]{1,0:T(8,128)(2,1)}, u32[]{:S(2)}, u32[]{:S(2)}) %collective-permute-start.15) | collective-permute-done | bytes 524320 | tf_op jit(solution)/shard_map/ppermute | solution.py:54
  45.4 1.9 %collective-permute-start.8 = (bf16[2048,128]{1,0:T(8,128)(2,1)}, bf16[2048,128]{1,0:T(8,128)(2,1)}, u32[]{:S(2)}, u32[]{:S(2)}) collective-permute-start(bf16[2048,128]{1,0:T(8,128)(2,1)} %collective-permute-done.4.refs_2_), channel_id=1, source_target_pairs={{0,32},{8,40},{16,48},{24,56},{32,64},{40,72},{48,80},{56,88},{64,... | collective-permute-start | bytes 1572872 | tf_op jit(solution)/shard_map/ppermute | solution.py:54
  47.2 0.4 collective-permute-start.9
  48.1 7.1 %collective-permute-done.18.refs_14_ = bf16[2048,128]{1,0:T(8,128)(2,1)} collective-permute-done((bf16[2048,128]{1,0:T(8,128)(2,1)}, bf16[2048,128]{1,0:T(8,128)(2,1)}, u32[]{:S(2)}, u32[]{:S(2)}) %collective-permute-start.18) | collective-permute-done | bytes 524320 | tf_op jit(solution)/shard_map/ppermute | solution.py:54
  55.2 1.0 collective-permute-done.8.refs_6_
  56.1 0.6 collective-permute-done.19.refs_15_
  56.7 2.0 %collective-permute-done.9.refs_7_ = bf16[2048,128]{1,0:T(8,128)(2,1)} collective-permute-done((bf16[2048,128]{1,0:T(8,128)(2,1)}, bf16[2048,128]{1,0:T(8,128)(2,1)}, u32[]{:S(2)}, u32[]{:S(2)}) %collective-permute-start.9) | collective-permute-done | bytes 524320 | tf_op jit(solution)/shard_map/ppermute | solution.py:54
  58.7 14.3 %attend_first.1 = (bf16[512,1024]{1,0:T(8,128)(2,1)S(1)}, bf16[16384,128]{1,0:T(8,128)(2,1)}, bf16[16384,128]{1,0:T(8,128)(2,1)}) custom-call(s32[1088]{0:T(1024)S(1)} %concatenate.21.tab, bf16[512,1024]{1,0:T(8,128)(2,1)S(1)} %get-tuple-element.54.q_ref, bf16[2048,128]{1,0:T(8,128)(2,1)} %copy-done.4, ...), custom_call_target="tpu_custom_call" | custom-call | flops 8589934592 | bytes 5242880 | tf_op jit(solution)/shard_map/attend_first/pallas_call | solution.py:181
  73.3 2.5 %collective-permute-done.20.refs_1_.refs_3_ = bf16[512,1024]{1,0:T(8,128)(2,1)S(1)} collective-permute-done((bf16[512,1024]{1,0:T(8,128)(2,1)S(1)}, bf16[512,1024]{1,0:T(8,128)(2,1)S(1)}, u32[]{:S(2)}, u32[]{:S(2)}) %collective-permute-start.20) | collective-permute-done | bytes 1048608 | tf_op jit(solution)/shard_map/ppermute | solution.py:369
  75.8 10.3 %product.3 = (bf16[512,1024]{1,0:T(8,128)(2,1)S(1)}, bf16[512,1024]{1,0:T(8,128)(2,1)S(1)}, f32[256,1024]{1,0:T(8,128)S(1)}, f32[256,1024]{1,0:T(8,128)S(1)}) custom-call(s32[4]{0:T(128)S(1)} %pad_add_fusion.cols, bf16[512,1024]{1,0:T(8,128)(2,1)S(1)} %get-tuple-element.28.refs_0_.refs_2_, bf16[512,1024]{1,0:T(8,128)(2,1)S(1)} %collective-permute-done.20.refs_1_.refs_3_, ...), custom_call_target="tpu_custom_call" | custom-call | flops 25769803776 | bytes 8388608 | tf_op jit(solution)/shard_map/product/pallas_call | solution.py:304
  86.1 0.7 collective-permute-start.22
  86.8 2.6 %collective-permute-start.23 = (bf16[512,1024]{1,0:T(8,128)(2,1)S(1)}, bf16[512,1024]{1,0:T(8,128)(2,1)S(1)}, u32[]{:S(2)}, u32[]{:S(2)}) collective-permute-start(bf16[512,1024]{1,0:T(8,128)(2,1)S(1)} %get-tuple-element.35), channel_id=1, source_target_pairs={{0,6},{1,7},{2,0},{3,1},{4,2},{5,3},{6,4},{7,5},{8,14},{9,15},{10,... | collective-permute-start | bytes 3145736 | tf_op jit(solution)/shard_map/ppermute | solution.py:345
  89.4 11.5 %attend.1.refs_0_ = bf16[512,1024]{1,0:T(8,128)(2,1)S(1)} custom-call(s32[1088]{0:T(1024)S(1)} %concatenate.22.tab, bf16[512,1024]{1,0:T(8,128)(2,1)S(1)} %get-tuple-element.53.q_ref, bf16[16384,128]{1,0:T(8,128)(2,1)S(1)} %copy-done, bf16[16384,128]{1,0:T(8,128)(2,1)S(1)} %copy-done.1), custom_call_target="tpu_custom_call" | custom-call | flops 8589934592 | bytes 5242880 | tf_op jit(solution)/shard_map/attend/pallas_call | solution.py:191
  101.0 11.6 %collective-permute-done.22 = bf16[512,1024]{1,0:T(8,128)(2,1)S(1)} collective-permute-done((bf16[512,1024]{1,0:T(8,128)(2,1)S(1)}, bf16[512,1024]{1,0:T(8,128)(2,1)S(1)}, u32[]{:S(2)}, u32[]{:S(2)}) %collective-permute-start.22) | collective-permute-done | bytes 1048608 | tf_op jit(solution)/shard_map/ppermute | solution.py:345
  113.3 3.3 %collective-permute-start.26 = (bf16[256,1024]{1,0:T(8,128)(2,1)S(1)}, bf16[256,1024]{1,0:T(8,128)(2,1)S(1)}, u32[]{:S(2)}, u32[]{:S(2)}) collective-permute-start(bf16[256,1024]{1,0:T(8,128)(2,1)S(1)} %add_convert_fusion.4), channel_id=1, source_target_pairs={{0,6},{1,7},{2,0},{3,1},{4,2},{5,3},{6,4},{7,5},{8,14},{9,15},{10,... | collective-permute-start | bytes 1572872 | tf_op jit(solution)/shard_map/ppermute | solution.py:345
  116.5 12.7 %product.4 = (bf16[512,1024]{1,0:T(8,128)(2,1)S(1)}, bf16[512,1024]{1,0:T(8,128)(2,1)S(1)}, f32[256,1024]{1,0:T(8,128)S(1)}, f32[256,1024]{1,0:T(8,128)S(1)}, f32[512,1024]{1,0:T(8,128)S(1)}) custom-call(s32[4]{0:T(128)S(1)} %pad_add_fusion.cols, bf16[512,1024]{1,0:T(8,128)(2,1)S(1)} %attend.1.refs_0_, ...), custom_call_target="tpu_custom_call" | custom-call | flops 34359738368 | bytes 10485760 | tf_op jit(solution)/shard_map/product/pallas_call | solution.py:304
  129.3 3.2 %collective-permute-start.29 = (bf16[512,1024]{1,0:T(8,128)(2,1)S(1)}, bf16[512,1024]{1,0:T(8,128)(2,1)S(1)}, u32[]{:S(2)}, u32[]{:S(2)}) collective-permute-start(bf16[512,1024]{1,0:T(8,128)(2,1)S(1)} %get-tuple-element.42), channel_id=1, source_target_pairs={{0,6},{1,7},{2,0},{3,1},{4,2},{5,3},{6,4},{7,5},{8,14},{9,15},{10,... | collective-permute-start | bytes 3145736 | tf_op jit(solution)/shard_map/ppermute | solution.py:345
  132.5 5.1 %product.5 = f32[512,1024]{1,0:T(8,128)S(1)} custom-call(s32[4]{0:T(128)S(1)} %pad_add_fusion.cols, bf16[512,1024]{1,0:T(8,128)(2,1)S(1)} %attend.1.refs_0_, bf16[512,1024]{1,0:T(8,128)(2,1)S(1)} %collective-permute-done.24.refs_1_, bf16[1024,8192]{1,0:T(8,128)(2,1)} %refs_2_.3, bf16[1024,8192]{1,0:T(8,128)(2,1)} %collective-permute-done.21.refs_3_.refs_5_), custom_call_target="tpu_custom_call" | custom-call | flops 8589934592 | bytes 4194304 | tf_op jit(solution)/shard_map/product/pallas_call | solution.py:304
  137.6 16.7 %collective-permute-done.27 = bf16[512,1024]{1,0:T(8,128)(2,1)S(1)} collective-permute-done((bf16[512,1024]{1,0:T(8,128)(2,1)S(1)}, bf16[512,1024]{1,0:T(8,128)(2,1)S(1)}, u32[]{:S(2)}, u32[]{:S(2)}) %collective-permute-start.27) | collective-permute-done | bytes 1048608 | tf_op jit(solution)/shard_map/ppermute | solution.py:345
  154.7 3.3 %collective-permute-start.30 = (bf16[256,1024]{1,0:T(8,128)(2,1)S(1)}, bf16[256,1024]{1,0:T(8,128)(2,1)S(1)}, u32[]{:S(2)}, u32[]{:S(2)}) collective-permute-start(bf16[256,1024]{1,0:T(8,128)(2,1)S(1)} %add_convert_fusion), channel_id=1, source_target_pairs={{0,6},{1,7},{2,0},{3,1},{4,2},{5,3},{6,4},{7,5},{8,14},{9,15},{10,... | collective-permute-start | bytes 1572872 | tf_op jit(solution)/shard_map/ppermute | solution.py:345
  158.0 0.5 add_convert_fusion.3
  158.6 8.8 %collective-permute-done.28 = bf16[256,1024]{1,0:T(8,128)(2,1)S(1)} collective-permute-done((bf16[256,1024]{1,0:T(8,128)(2,1)S(1)}, bf16[256,1024]{1,0:T(8,128)(2,1)S(1)}, u32[]{:S(2)}, u32[]{:S(2)}) %collective-permute-start.28) | collective-permute-done | bytes 524320 | tf_op jit(solution)/shard_map/ppermute | solution.py:345
  167.4 0.6 fusion.3
  168.0 1.5 pad_maximum_fusion
  (83 shorter events, 4.4 us)
Async XLA Ops:
  0.0 75.8 %collective-permute-start.21 = (bf16[1024,8192]{1,0:T(8,128)(2,1)}, bf16[1024,8192]{1,0:T(8,128)(2,1)}, u32[]{:S(2)}, u32[]{:S(2)}) collective-permute-start(bf16[1024,8192]{1,0:T(8,128)(2,1)} %refs_2_.3), channel_id=1, source_target_pairs={{0,1},{1,0},{2,3},{3,2},{4,5},{5,4},{6,7},{7,6},{8,9},{9,8},{10,11... | collective-permute-start | bytes 50331656 | tf_op jit(solution)/shard_map/ppermute | solution.py:342
  0.0 10.2 %collective-permute-start = (bf16[1024,128]{1,0:T(8,128)(2,1)}, bf16[1024,128]{1,0:T(8,128)(2,1)S(1)}, u32[]{:S(2)}, u32[]{:S(2)}) collective-permute-start(bf16[1024,128]{1,0:T(8,128)(2,1)} %param.8), channel_id=1, source_target_pairs={{0,8},{8,16},{16,24},{24,0},{32,40},{40,48},{48,56},{56,32},{64,72... | collective-permute-start | bytes 786440 | tf_op jit(solution)/shard_map/ppermute | solution.py:41
  1.5 9.1 %collective-permute-start.1 = (bf16[1024,128]{1,0:T(8,128)(2,1)}, bf16[1024,128]{1,0:T(8,128)(2,1)S(1)}, u32[]{:S(2)}, u32[]{:S(2)}) collective-permute-start(bf16[1024,128]{1,0:T(8,128)(2,1)} %param.8), channel_id=1, source_target_pairs={{0,24},{8,0},{16,8},{24,16},{32,56},{40,32},{48,40},{56,48},{64,88... | collective-permute-start | bytes 786440 | tf_op jit(solution)/shard_map/ppermute | solution.py:42
  3.2 10.4 %collective-permute-start.10 = (bf16[1024,128]{1,0:T(8,128)(2,1)}, bf16[1024,128]{1,0:T(8,128)(2,1)S(1)}, u32[]{:S(2)}, u32[]{:S(2)}) collective-permute-start(bf16[1024,128]{1,0:T(8,128)(2,1)} %param.9), channel_id=1, source_target_pairs={{0,32},{8,40},{16,48},{24,56},{32,64},{40,72},{48,80},{56,88},{64,... | collective-permute-start | bytes 786440 | tf_op jit(solution)/shard_map/ppermute | solution.py:41
  3.2 11.7 %collective-permute-start.11 = (bf16[1024,128]{1,0:T(8,128)(2,1)}, bf16[1024,128]{1,0:T(8,128)(2,1)S(1)}, u32[]{:S(2)}, u32[]{:S(2)}) collective-permute-start(bf16[1024,128]{1,0:T(8,128)(2,1)} %param.9), channel_id=1, source_target_pairs={{0,96},{8,104},{16,112},{24,120},{32,0},{40,8},{48,16},{56,24},{64... | collective-permute-start | bytes 786440 | tf_op jit(solution)/shard_map/ppermute | solution.py:42
  10.3 6.4 %collective-permute-start.2 = (bf16[512,128]{1,0:T(8,128)(2,1)S(1)}, bf16[512,128]{1,0:T(8,128)(2,1)S(1)}, u32[]{:S(2)}, u32[]{:S(2)}) collective-permute-start(bf16[512,128]{1,0:T(8,128)(2,1)S(1)} %slice.132), channel_id=1, source_target_pairs={{0,8},{8,16},{16,24},{24,0},{32,40},{40,48},{48,56},{56,32},{64,72... | collective-permute-start | bytes 393224 | tf_op jit(solution)/shard_map/ppermute | solution.py:43
  10.6 6.5 %collective-permute-start.3 = (bf16[512,128]{1,0:T(8,128)(2,1)S(1)}, bf16[512,128]{1,0:T(8,128)(2,1)S(1)}, u32[]{:S(2)}, u32[]{:S(2)}) collective-permute-start(bf16[512,128]{1,0:T(8,128)(2,1)S(1)} %slice.133), channel_id=1, source_target_pairs={{0,24},{8,0},{16,8},{24,16},{32,56},{40,32},{48,40},{56,48},{64,88... | collective-permute-start | bytes 393224 | tf_op jit(solution)/shard_map/ppermute | solution.py:44
  13.7 5.1 %collective-permute-start.12 = (bf16[512,128]{1,0:T(8,128)(2,1)S(1)}, bf16[512,128]{1,0:T(8,128)(2,1)S(1)}, u32[]{:S(2)}, u32[]{:S(2)}) collective-permute-start(bf16[512,128]{1,0:T(8,128)(2,1)S(1)} %slice.134), channel_id=1, source_target_pairs={{0,32},{8,40},{16,48},{24,56},{32,64},{40,72},{48,80},{56,88},{64,... | collective-permute-start | bytes 393224 | tf_op jit(solution)/shard_map/ppermute | solution.py:43
  15.0 32.9 %copy-start.2 = (bf16[1024,1024]{1,0:T(8,128)(2,1)S(1)}, bf16[1024,1024]{1,0:T(8,128)(2,1)}, u32[]{:S(2)}) copy-start(bf16[1024,1024]{1,0:T(8,128)(2,1)} %param.7) | copy-start | bytes 6291460
  15.0 7.0 %collective-permute-start.13 = (bf16[512,128]{1,0:T(8,128)(2,1)S(1)}, bf16[512,128]{1,0:T(8,128)(2,1)S(1)}, u32[]{:S(2)}, u32[]{:S(2)}) collective-permute-start(bf16[512,128]{1,0:T(8,128)(2,1)S(1)} %slice.135), channel_id=1, source_target_pairs={{0,96},{8,104},{16,112},{24,120},{32,0},{40,8},{48,16},{56,24},{64... | collective-permute-start | bytes 393224 | tf_op jit(solution)/shard_map/ppermute | solution.py:44
  16.6 14.5 %copy-start.4 = (bf16[2048,128]{1,0:T(8,128)(2,1)}, bf16[2048,128]{1,0:T(8,128)(2,1)S(1)}, u32[]{:S(2)}) copy-start(bf16[2048,128]{1,0:T(8,128)(2,1)S(1)} %constant_dynamic-update-slice_fusion.refs_0_) | copy-start | bytes 1572868
  16.7 5.4 %copy-start.3 = (bf16[2048,128]{1,0:T(8,128)(2,1)}, bf16[2048,128]{1,0:T(8,128)(2,1)S(1)}, u32[]{:S(2)}) copy-start(bf16[2048,128]{1,0:T(8,128)(2,1)S(1)} %constant_dynamic-update-slice_fusion.5.refs_8_) | copy-start | bytes 1572868
  16.7 12.4 %collective-permute-start.16 = (bf16[2048,128]{1,0:T(8,128)(2,1)S(1)}, bf16[2048,128]{1,0:T(8,128)(2,1)S(1)}, u32[]{:S(2)}, u32[]{:S(2)}) collective-permute-start(bf16[2048,128]{1,0:T(8,128)(2,1)S(1)} %constant_dynamic-update-slice_fusion.5.refs_8_), channel_id=1, source_target_pairs={{0,24},{8,0},{16,8},{24,16},{32,56},{40,32},{48,40},{56,48},{64,88... | collective-permute-start | bytes 1572872 | tf_op jit(solution)/shard_map/ppermute | solution.py:54
  17.1 14.0 %collective-permute-start.14 = (bf16[2048,128]{1,0:T(8,128)(2,1)S(1)}, bf16[2048,128]{1,0:T(8,128)(2,1)}, u32[]{:S(2)}, u32[]{:S(2)}) collective-permute-start(bf16[2048,128]{1,0:T(8,128)(2,1)S(1)} %constant_dynamic-update-slice_fusion.5.refs_8_), channel_id=1, source_target_pairs={{0,8},{8,16},{16,24},{24,0},{32,40},{40,48},{48,56},{56,32},{64,72... | collective-permute-start | bytes 1572872 | tf_op jit(solution)/shard_map/ppermute | solution.py:54
  18.8 13.7 %collective-permute-start.6 = (bf16[2048,128]{1,0:T(8,128)(2,1)S(1)}, bf16[2048,128]{1,0:T(8,128)(2,1)S(1)}, u32[]{:S(2)}, u32[]{:S(2)}) collective-permute-start(bf16[2048,128]{1,0:T(8,128)(2,1)S(1)} %constant_dynamic-update-slice_fusion.refs_0_), channel_id=1, source_target_pairs={{0,96},{8,104},{16,112},{24,120},{32,0},{40,8},{48,16},{56,24},{64... | collective-permute-start | bytes 1572872 | tf_op jit(solution)/shard_map/ppermute | solution.py:54
  22.0 10.9 %collective-permute-start.4 = (bf16[2048,128]{1,0:T(8,128)(2,1)S(1)}, bf16[2048,128]{1,0:T(8,128)(2,1)}, u32[]{:S(2)}, u32[]{:S(2)}) collective-permute-start(bf16[2048,128]{1,0:T(8,128)(2,1)S(1)} %constant_dynamic-update-slice_fusion.refs_0_), channel_id=1, source_target_pairs={{0,32},{8,40},{16,48},{24,56},{32,64},{40,72},{48,80},{56,88},{64,... | collective-permute-start | bytes 1572872 | tf_op jit(solution)/shard_map/ppermute | solution.py:54
  23.4 24.4 %copy-start.5 = (bf16[2048,128]{1,0:T(8,128)(2,1)}, bf16[2048,128]{1,0:T(8,128)(2,1)S(1)}, u32[]{:S(2)}) copy-start(bf16[2048,128]{1,0:T(8,128)(2,1)S(1)} %constant_dynamic-update-slice_fusion.7.refs_9_) | copy-start | bytes 1572868
  29.1 6.7 %copy-start.6 = (bf16[2048,128]{1,0:T(8,128)(2,1)}, bf16[2048,128]{1,0:T(8,128)(2,1)S(1)}, u32[]{:S(2)}) copy-start(bf16[2048,128]{1,0:T(8,128)(2,1)S(1)} %collective-permute-done.16.refs_12_) | copy-start | bytes 1572868
  29.1 11.6 %collective-permute-start.17 = (bf16[2048,128]{1,0:T(8,128)(2,1)S(1)}, bf16[2048,128]{1,0:T(8,128)(2,1)}, u32[]{:S(2)}, u32[]{:S(2)}) collective-permute-start(bf16[2048,128]{1,0:T(8,128)(2,1)S(1)} %constant_dynamic-update-slice_fusion.7.refs_9_), channel_id=1, source_target_pairs={{0,24},{8,0},{16,8},{24,16},{32,56},{40,32},{48,40},{56,48},{64,88... | collective-permute-start | bytes 1572872 | tf_op jit(solution)/shard_map/ppermute | solution.py:54
  31.1 14.3 %collective-permute-start.15 = (bf16[2048,128]{1,0:T(8,128)(2,1)S(1)}, bf16[2048,128]{1,0:T(8,128)(2,1)}, u32[]{:S(2)}, u32[]{:S(2)}) collective-permute-start(bf16[2048,128]{1,0:T(8,128)(2,1)S(1)} %constant_dynamic-update-slice_fusion.7.refs_9_), channel_id=1, source_target_pairs={{0,8},{8,16},{16,24},{24,0},{32,40},{40,48},{48,56},{56,32},{64,72... | collective-permute-start | bytes 1572872 | tf_op jit(solution)/shard_map/ppermute | solution.py:54
  32.5 3.3 %copy-start.7 = (bf16[2048,128]{1,0:T(8,128)(2,1)}, bf16[2048,128]{1,0:T(8,128)(2,1)S(1)}, u32[]{:S(2)}) copy-start(bf16[2048,128]{1,0:T(8,128)(2,1)S(1)} %collective-permute-done.6.refs_4_) | copy-start | bytes 1572868
  32.5 14.7 %collective-permute-start.7 = (bf16[2048,128]{1,0:T(8,128)(2,1)}, bf16[2048,128]{1,0:T(8,128)(2,1)}, u32[]{:S(2)}, u32[]{:S(2)}) collective-permute-start(bf16[2048,128]{1,0:T(8,128)(2,1)} %constant_dynamic-update-slice_fusion.2.refs_1_), channel_id=1, source_target_pairs={{0,96},{8,104},{16,112},{24,120},{32,0},{40,8},{48,16},{56,24},{64... | collective-permute-start | bytes 1572872 | tf_op jit(solution)/shard_map/ppermute | solution.py:54
  32.8 14.4 %collective-permute-start.5 = (bf16[2048,128]{1,0:T(8,128)(2,1)}, bf16[2048,128]{1,0:T(8,128)(2,1)}, u32[]{:S(2)}, u32[]{:S(2)}) collective-permute-start(bf16[2048,128]{1,0:T(8,128)(2,1)} %constant_dynamic-update-slice_fusion.2.refs_1_), channel_id=1, source_target_pairs={{0,32},{8,40},{16,48},{24,56},{32,64},{40,72},{48,80},{56,88},{64,... | collective-permute-start | bytes 1572872 | tf_op jit(solution)/shard_map/ppermute | solution.py:54
  40.7 14.5 %collective-permute-start.18 = (bf16[2048,128]{1,0:T(8,128)(2,1)}, bf16[2048,128]{1,0:T(8,128)(2,1)}, u32[]{:S(2)}, u32[]{:S(2)}) collective-permute-start(bf16[2048,128]{1,0:T(8,128)(2,1)} %collective-permute-done.14.refs_10_), channel_id=1, source_target_pairs={{0,8},{8,16},{16,24},{24,0},{32,40},{40,48},{48,56},{56,32},{64,72... | collective-permute-start | bytes 1572872 | tf_op jit(solution)/shard_map/ppermute | solution.py:54
  45.4 10.8 %collective-permute-start.8 = (bf16[2048,128]{1,0:T(8,128)(2,1)}, bf16[2048,128]{1,0:T(8,128)(2,1)}, u32[]{:S(2)}, u32[]{:S(2)}) collective-permute-start(bf16[2048,128]{1,0:T(8,128)(2,1)} %collective-permute-done.4.refs_2_), channel_id=1, source_target_pairs={{0,32},{8,40},{16,48},{24,56},{32,64},{40,72},{48,80},{56,88},{64,... | collective-permute-start | bytes 1572872 | tf_op jit(solution)/shard_map/ppermute | solution.py:54
  47.2 9.5 %collective-permute-start.19 = (bf16[2048,128]{1,0:T(8,128)(2,1)}, bf16[2048,128]{1,0:T(8,128)(2,1)}, u32[]{:S(2)}, u32[]{:S(2)}) collective-permute-start(bf16[2048,128]{1,0:T(8,128)(2,1)} %collective-permute-done.17.refs_13_), channel_id=1, source_target_pairs={{0,24},{8,0},{16,8},{24,16},{32,56},{40,32},{48,40},{56,48},{64,88... | collective-permute-start | bytes 1572872 | tf_op jit(solution)/shard_map/ppermute | solution.py:54
  47.2 11.5 %collective-permute-start.9 = (bf16[2048,128]{1,0:T(8,128)(2,1)}, bf16[2048,128]{1,0:T(8,128)(2,1)}, u32[]{:S(2)}, u32[]{:S(2)}) collective-permute-start(bf16[2048,128]{1,0:T(8,128)(2,1)} %collective-permute-done.7.refs_5_), channel_id=1, source_target_pairs={{0,96},{8,104},{16,112},{24,120},{32,0},{40,8},{48,16},{56,24},{64... | collective-permute-start | bytes 1572872 | tf_op jit(solution)/shard_map/ppermute | solution.py:54
  73.1 2.7 %collective-permute-start.20 = (bf16[512,1024]{1,0:T(8,128)(2,1)S(1)}, bf16[512,1024]{1,0:T(8,128)(2,1)S(1)}, u32[]{:S(2)}, u32[]{:S(2)}) collective-permute-start(bf16[512,1024]{1,0:T(8,128)(2,1)S(1)} %get-tuple-element.28.refs_0_.refs_2_), channel_id=1, source_target_pairs={{0,1},{1,0},{2,3},{3,2},{4,5},{5,4},{6,7},{7,6},{8,9},{9,8},{10,11... | collective-permute-start | bytes 3145736 | tf_op jit(solution)/shard_map/ppermute | solution.py:369
  73.3 16.1 %copy-start = (bf16[16384,128]{1,0:T(8,128)(2,1)S(1)}, bf16[16384,128]{1,0:T(8,128)(2,1)}, u32[]{:S(2)}) copy-start(bf16[16384,128]{1,0:T(8,128)(2,1)} %get-tuple-element.31.k_all) | copy-start | bytes 12582916
  73.3 16.1 %copy-start.1 = (bf16[16384,128]{1,0:T(8,128)(2,1)S(1)}, bf16[16384,128]{1,0:T(8,128)(2,1)}, u32[]{:S(2)}) copy-start(bf16[16384,128]{1,0:T(8,128)(2,1)} %get-tuple-element.32.v_all) | copy-start | bytes 12582916
  86.1 26.5 %collective-permute-start.22 = (bf16[512,1024]{1,0:T(8,128)(2,1)S(1)}, bf16[512,1024]{1,0:T(8,128)(2,1)S(1)}, u32[]{:S(2)}, u32[]{:S(2)}) collective-permute-start(bf16[512,1024]{1,0:T(8,128)(2,1)S(1)} %get-tuple-element.33), channel_id=1, source_target_pairs={{0,2},{1,3},{2,4},{3,5},{4,6},{5,7},{6,0},{7,1},{8,10},{9,11},{10,... | collective-permute-start | bytes 3145736 | tf_op jit(solution)/shard_map/ppermute | solution.py:345
  86.8 26.3 %collective-permute-start.23 = (bf16[512,1024]{1,0:T(8,128)(2,1)S(1)}, bf16[512,1024]{1,0:T(8,128)(2,1)S(1)}, u32[]{:S(2)}, u32[]{:S(2)}) collective-permute-start(bf16[512,1024]{1,0:T(8,128)(2,1)S(1)} %get-tuple-element.35), channel_id=1, source_target_pairs={{0,6},{1,7},{2,0},{3,1},{4,2},{5,3},{6,4},{7,5},{8,14},{9,15},{10,... | collective-permute-start | bytes 3145736 | tf_op jit(solution)/shard_map/ppermute | solution.py:345
  100.9 15.6 %collective-permute-start.24 = (bf16[512,1024]{1,0:T(8,128)(2,1)S(1)}, bf16[512,1024]{1,0:T(8,128)(2,1)S(1)}, u32[]{:S(2)}, u32[]{:S(2)}) collective-permute-start(bf16[512,1024]{1,0:T(8,128)(2,1)S(1)} %attend.1.refs_0_), channel_id=1, source_target_pairs={{0,1},{1,0},{2,3},{3,2},{4,5},{5,4},{6,7},{7,6},{8,9},{9,8},{10,11... | collective-permute-start | bytes 3145736 | tf_op jit(solution)/shard_map/ppermute | solution.py:369
  112.7 19.8 %collective-permute-start.25 = (bf16[256,1024]{1,0:T(8,128)(2,1)S(1)}, bf16[256,1024]{1,0:T(8,128)(2,1)S(1)}, u32[]{:S(2)}, u32[]{:S(2)}) collective-permute-start(bf16[256,1024]{1,0:T(8,128)(2,1)S(1)} %add_convert_fusion.5), channel_id=1, source_target_pairs={{0,2},{1,3},{2,4},{3,5},{4,6},{5,7},{6,0},{7,1},{8,10},{9,11},{10,... | collective-permute-start | bytes 1572872 | tf_op jit(solution)/shard_map/ppermute | solution.py:345
  113.3 19.3 %collective-permute-start.26 = (bf16[256,1024]{1,0:T(8,128)(2,1)S(1)}, bf16[256,1024]{1,0:T(8,128)(2,1)S(1)}, u32[]{:S(2)}, u32[]{:S(2)}) collective-permute-start(bf16[256,1024]{1,0:T(8,128)(2,1)S(1)} %add_convert_fusion.4), channel_id=1, source_target_pairs={{0,6},{1,7},{2,0},{3,1},{4,2},{5,3},{6,4},{7,5},{8,14},{9,15},{10,... | collective-permute-start | bytes 1572872 | tf_op jit(solution)/shard_map/ppermute | solution.py:345
  129.2 25.1 %collective-permute-start.27 = (bf16[512,1024]{1,0:T(8,128)(2,1)S(1)}, bf16[512,1024]{1,0:T(8,128)(2,1)S(1)}, u32[]{:S(2)}, u32[]{:S(2)}) collective-permute-start(bf16[512,1024]{1,0:T(8,128)(2,1)S(1)} %get-tuple-element.41), channel_id=1, source_target_pairs={{0,2},{1,3},{2,4},{3,5},{4,6},{5,7},{6,0},{7,1},{8,10},{9,11},{10,... | collective-permute-start | bytes 3145736 | tf_op jit(solution)/shard_map/ppermute | solution.py:345
  129.3 25.3 %collective-permute-start.29 = (bf16[512,1024]{1,0:T(8,128)(2,1)S(1)}, bf16[512,1024]{1,0:T(8,128)(2,1)S(1)}, u32[]{:S(2)}, u32[]{:S(2)}) collective-permute-start(bf16[512,1024]{1,0:T(8,128)(2,1)S(1)} %get-tuple-element.42), channel_id=1, source_target_pairs={{0,6},{1,7},{2,0},{3,1},{4,2},{5,3},{6,4},{7,5},{8,14},{9,15},{10,... | collective-permute-start | bytes 3145736 | tf_op jit(solution)/shard_map/ppermute | solution.py:345
  154.5 12.9 %collective-permute-start.28 = (bf16[256,1024]{1,0:T(8,128)(2,1)S(1)}, bf16[256,1024]{1,0:T(8,128)(2,1)S(1)}, u32[]{:S(2)}, u32[]{:S(2)}) collective-permute-start(bf16[256,1024]{1,0:T(8,128)(2,1)S(1)} %add_convert_fusion.1), channel_id=1, source_target_pairs={{0,2},{1,3},{2,4},{3,5},{4,6},{5,7},{6,0},{7,1},{8,10},{9,11},{10,... | collective-permute-start | bytes 1572872 | tf_op jit(solution)/shard_map/ppermute | solution.py:345
  154.7 12.7 %collective-permute-start.30 = (bf16[256,1024]{1,0:T(8,128)(2,1)S(1)}, bf16[256,1024]{1,0:T(8,128)(2,1)S(1)}, u32[]{:S(2)}, u32[]{:S(2)}) collective-permute-start(bf16[256,1024]{1,0:T(8,128)(2,1)S(1)} %add_convert_fusion), channel_id=1, source_target_pairs={{0,6},{1,7},{2,0},{3,1},{4,2},{5,3},{6,4},{7,5},{8,14},{9,15},{10,... | collective-permute-start | bytes 1572872 | tf_op jit(solution)/shard_map/ppermute | solution.py:345

commit v3 on v2

--- a/solution.py
+++ b/solution.py
@@ -14,7 +14,7 @@
 CORES = 2
 PARTS = 8
 CHUNKS = (4, 4)
-VARIANTS = (1, 2, 3, 4, 6, 8)
+VARIANTS = (1, 2, 3, 4, 5, 6, 8)
 ORDER = (2, 1, 3, 0)
 COST = 2
 NEG = -1e30

time: 171 us -> 171 us (level)
  waiting for transfers between devices: 66.6 us -> 68.4 us
  Pallas kernels: 53.9 us -> 52.1 us
    ppermute x8, waiting for transfers between devices: 37.3 us -> 39.1 us  [send(): return lax.ppermute(piece, 'tensor', along_y(step))]
  transfers between devices with their start and end apart: 31 -> 31, of which waited for: 15 -> 14; matrix products, arithmetic and copies ran while one was open for 7% -> 7% of each run, Pallas kernels for 26% -> 25%
where the time goes in v3:
time: 171 us; the launch traced here: 170 us
  waiting for transfers between devices  68.4 us (40%)
  Pallas kernels  52.1 us (30%)
  starting transfers between devices  34.5 us (20%)
  other arithmetic  8.5 us (5%)
  local copies, waits for them, and re-layouts  6.04 us (4%)
    ppermute x8, waiting for transfers between devices, send(): return lax.ppermute(piece, 'tensor', along_y(step))  39.1 us
    pallas_call x3, Pallas kernels, product(): pl.pallas_call(functools.partial(product_kernel, sends, owns), out_shape=...  28.1 us
    ppermute x12, waiting for transfers between devices, pass_on(): return lax.ppermute(part, 'seq', second(step))  24 us
    pallas_call x1, Pallas kernels, attend(): pl.pallas_call(functools.partial(attend_first_kernel, kmax), out_shape=[o...  13.8 us
    ppermute x8, starting transfers between devices, send(): return lax.ppermute(piece, 'tensor', along_y(step))  13.7 us
    pallas_call x1, Pallas kernels, attend(): pl.pallas_call(functools.partial(attend_kernel, kmax), out_shape=out, in_...  10.2 us
    ppermute x12, starting transfers between devices, pass_on(): return lax.ppermute(part, 'seq', second(step))  9.75 us
    ppermute x2, starting transfers between devices, ring(): far_high = lax.ppermute(after[half:], 'seq', perm(-1))  3.91 us
  transfers between devices with their start and end apart: 31, of which 14 were waited for; matrix products, arithmetic and copies ran while one was open for 7% of the time, Pallas kernels for 25%

profile of v3, /device:TPU:96, one launch (start us, length us, event | category | flops | bytes accessed | tf_op | source)
XLA Modules:
  0.0 169.9 jit_solution(15429772998380864330)
XLA Ops:
  0.0 1.5 collective-permute-start
  1.5 1.7 %collective-permute-start.1 = (bf16[1024,128]{1,0:T(8,128)(2,1)}, bf16[1024,128]{1,0:T(8,128)(2,1)S(1)}, u32[]{:S(2)}, u32[]{:S(2)}) collective-permute-start(bf16[1024,128]{1,0:T(8,128)(2,1)} %param.8), channel_id=1, source_target_pairs={{0,24},{8,0},{16,8},{24,16},{32,56},{40,32},{48,40},{56,48},{64,88... | collective-permute-start | bytes 786440 | tf_op jit(solution)/shard_map/ppermute | solution.py:42
  3.2 2.0 %collective-permute-start.11 = (bf16[1024,128]{1,0:T(8,128)(2,1)}, bf16[1024,128]{1,0:T(8,128)(2,1)S(1)}, u32[]{:S(2)}, u32[]{:S(2)}) collective-permute-start(bf16[1024,128]{1,0:T(8,128)(2,1)} %param.9), channel_id=1, source_target_pairs={{0,96},{8,104},{16,112},{24,120},{32,0},{40,8},{48,16},{56,24},{64... | collective-permute-start | bytes 786440 | tf_op jit(solution)/shard_map/ppermute | solution.py:42
  5.3 1.0 constant_dynamic-update-slice_fusion.1
  6.2 1.0 constant_dynamic-update-slice_fusion.6
  7.2 0.8 fusion.11
  8.0 1.1 add_bitcast_fusion
  9.1 1.1 add_bitcast_fusion.1
  10.6 3.0 %collective-permute-start.3 = (bf16[512,128]{1,0:T(8,128)(2,1)S(1)}, bf16[512,128]{1,0:T(8,128)(2,1)S(1)}, u32[]{:S(2)}, u32[]{:S(2)}) collective-permute-start(bf16[512,128]{1,0:T(8,128)(2,1)S(1)} %slice.133), channel_id=1, source_target_pairs={{0,24},{8,0},{16,8},{24,16},{32,56},{40,32},{48,40},{56,48},{64,88... | collective-permute-start | bytes 393224 | tf_op jit(solution)/shard_map/ppermute | solution.py:44
  13.7 1.3 collective-permute-start.12
  15.0 0.9 collective-permute-start.13
  15.9 0.7 constant_dynamic-update-slice_fusion.4
  16.7 0.4 collective-permute-start.16
  17.1 1.7 collective-permute-start.14
  19.2 2.8 %collective-permute-done.13 = bf16[512,128]{1,0:T(8,128)(2,1)S(1)} collective-permute-done((bf16[512,128]{1,0:T(8,128)(2,1)S(1)}, bf16[512,128]{1,0:T(8,128)(2,1)S(1)}, u32[]{:S(2)}, u32[]{:S(2)}) %collective-permute-start.13) | collective-permute-done | bytes 131104 | tf_op jit(solution)/shard_map/ppermute | solution.py:44
  22.1 0.7 constant_dynamic-update-slice_fusion.3
  22.7 0.7 constant_dynamic-update-slice_fusion.2.refs_1_
  23.4 5.6 %collective-permute-done.16.refs_12_ = bf16[2048,128]{1,0:T(8,128)(2,1)S(1)} collective-permute-done((bf16[2048,128]{1,0:T(8,128)(2,1)S(1)}, bf16[2048,128]{1,0:T(8,128)(2,1)S(1)}, u32[]{:S(2)}, u32[]{:S(2)}) %collective-permute-start.16) | collective-permute-done | bytes 524320 | tf_op jit(solution)/shard_map/ppermute | solution.py:54
  29.1 2.0 %collective-permute-start.17 = (bf16[2048,128]{1,0:T(8,128)(2,1)S(1)}, bf16[2048,128]{1,0:T(8,128)(2,1)}, u32[]{:S(2)}, u32[]{:S(2)}) collective-permute-start(bf16[2048,128]{1,0:T(8,128)(2,1)S(1)} %constant_dynamic-update-slice_fusion.7.refs_9_), channel_id=1, source_target_pairs={{0,24},{8,0},{16,8},{24,16},{32,56},{40,32},{48,40},{56,48},{64,88... | collective-permute-start | bytes 1572872 | tf_op jit(solution)/shard_map/ppermute | solution.py:54
  31.1 1.3 collective-permute-done.6.refs_4_
  32.8 2.9 %collective-permute-start.5 = (bf16[2048,128]{1,0:T(8,128)(2,1)}, bf16[2048,128]{1,0:T(8,128)(2,1)}, u32[]{:S(2)}, u32[]{:S(2)}) collective-permute-start(bf16[2048,128]{1,0:T(8,128)(2,1)} %constant_dynamic-update-slice_fusion.2.refs_1_), channel_id=1, source_target_pairs={{0,32},{8,40},{16,48},{24,56},{32,64},{40,72},{48,80},{56,88},{64,... | collective-permute-start | bytes 1572872 | tf_op jit(solution)/shard_map/ppermute | solution.py:54
  37.3 2.1 %sort.17 = (s32[64]{0:T(128)}, s32[64]{0:T(128)S(1)}) sort(s32[64]{0:T(128)S(1)} %reshape.13, s32[64]{0:T(128)S(1)} %iota.4), dimensions={0}, to_apply=%region_0.1 | sort | flops 384 | bytes 1024 | tf_op jit(solution)/shard_map/jit(argsort)/sort | solution.py:221
  39.4 1.3 collective-permute-done.17.refs_13_
  40.7 4.7 %collective-permute-done.15.refs_11_ = bf16[2048,128]{1,0:T(8,128)(2,1)} collective-permute-done((bf16[2048,128]{1,0:T(8,128)(2,1)S(1)}, bf16[2048,128]{1,0:T(8,128)(2,1)}, u32[]{:S(2)}, u32[]{:S(2)}) %collective-permute-start.15) | collective-permute-done | bytes 524320 | tf_op jit(solution)/shard_map/ppermute | solution.py:54
  45.4 1.9 %collective-permute-start.8 = (bf16[2048,128]{1,0:T(8,128)(2,1)}, bf16[2048,128]{1,0:T(8,128)(2,1)}, u32[]{:S(2)}, u32[]{:S(2)}) collective-permute-start(bf16[2048,128]{1,0:T(8,128)(2,1)} %collective-permute-done.4.refs_2_), channel_id=1, source_target_pairs={{0,32},{8,40},{16,48},{24,56},{32,64},{40,72},{48,80},{56,88},{64,... | collective-permute-start | bytes 1572872 | tf_op jit(solution)/shard_map/ppermute | solution.py:54
  47.2 0.4 collective-permute-start.9
  48.1 7.1 %collective-permute-done.18.refs_14_ = bf16[2048,128]{1,0:T(8,128)(2,1)} collective-permute-done((bf16[2048,128]{1,0:T(8,128)(2,1)}, bf16[2048,128]{1,0:T(8,128)(2,1)}, u32[]{:S(2)}, u32[]{:S(2)}) %collective-permute-start.18) | collective-permute-done | bytes 524320 | tf_op jit(solution)/shard_map/ppermute | solution.py:54
  55.2 1.0 collective-permute-done.8.refs_6_
  56.1 0.6 collective-permute-done.19.refs_15_
  56.7 2.0 %collective-permute-done.9.refs_7_ = bf16[2048,128]{1,0:T(8,128)(2,1)} collective-permute-done((bf16[2048,128]{1,0:T(8,128)(2,1)}, bf16[2048,128]{1,0:T(8,128)(2,1)}, u32[]{:S(2)}, u32[]{:S(2)}) %collective-permute-start.9) | collective-permute-done | bytes 524320 | tf_op jit(solution)/shard_map/ppermute | solution.py:54
  58.7 13.8 %attend_first.1 = (bf16[512,1024]{1,0:T(8,128)(2,1)S(1)}, bf16[16384,128]{1,0:T(8,128)(2,1)}, bf16[16384,128]{1,0:T(8,128)(2,1)}) custom-call(s32[1088]{0:T(1024)S(1)} %concatenate.21.tab, bf16[512,1024]{1,0:T(8,128)(2,1)S(1)} %get-tuple-element.54.q_ref, bf16[2048,128]{1,0:T(8,128)(2,1)} %copy-done.4, ...), custom_call_target="tpu_custom_call" | custom-call | flops 8589934592 | bytes 5242880 | tf_op jit(solution)/shard_map/attend_first/pallas_call | solution.py:181
  72.8 2.5 %collective-permute-done.20.refs_1_.refs_3_ = bf16[512,1024]{1,0:T(8,128)(2,1)S(1)} collective-permute-done((bf16[512,1024]{1,0:T(8,128)(2,1)S(1)}, bf16[512,1024]{1,0:T(8,128)(2,1)S(1)}, u32[]{:S(2)}, u32[]{:S(2)}) %collective-permute-start.20) | collective-permute-done | bytes 1048608 | tf_op jit(solution)/shard_map/ppermute | solution.py:369
  75.3 10.3 %product.3 = (bf16[512,1024]{1,0:T(8,128)(2,1)S(1)}, bf16[512,1024]{1,0:T(8,128)(2,1)S(1)}, f32[256,1024]{1,0:T(8,128)S(1)}, f32[256,1024]{1,0:T(8,128)S(1)}) custom-call(s32[4]{0:T(128)S(1)} %pad_add_fusion.cols, bf16[512,1024]{1,0:T(8,128)(2,1)S(1)} %get-tuple-element.28.refs_0_.refs_2_, bf16[512,1024]{1,0:T(8,128)(2,1)S(1)} %collective-permute-done.20.refs_1_.refs_3_, ...), custom_call_target="tpu_custom_call" | custom-call | flops 25769803776 | bytes 8388608 | tf_op jit(solution)/shard_map/product/pallas_call | solution.py:304
  85.6 1.8 %collective-permute-start.22 = (bf16[512,1024]{1,0:T(8,128)(2,1)S(1)}, bf16[512,1024]{1,0:T(8,128)(2,1)S(1)}, u32[]{:S(2)}, u32[]{:S(2)}) collective-permute-start(bf16[512,1024]{1,0:T(8,128)(2,1)S(1)} %get-tuple-element.33), channel_id=1, source_target_pairs={{0,2},{1,3},{2,4},{3,5},{4,6},{5,7},{6,0},{7,1},{8,10},{9,11},{10,... | collective-permute-start | bytes 3145736 | tf_op jit(solution)/shard_map/ppermute | solution.py:345
  87.4 1.6 collective-permute-start.23
  89.0 10.2 %attend.1.refs_0_ = bf16[512,1024]{1,0:T(8,128)(2,1)S(1)} custom-call(s32[1088]{0:T(1024)S(1)} %concatenate.22.tab, bf16[512,1024]{1,0:T(8,128)(2,1)S(1)} %get-tuple-element.53.q_ref, bf16[16384,128]{1,0:T(8,128)(2,1)S(1)} %copy-done, bf16[16384,128]{1,0:T(8,128)(2,1)S(1)} %copy-done.1), custom_call_target="tpu_custom_call" | custom-call | flops 8589934592 | bytes 5242880 | tf_op jit(solution)/shard_map/attend/pallas_call | solution.py:191
  99.4 13.0 %collective-permute-done.22 = bf16[512,1024]{1,0:T(8,128)(2,1)S(1)} collective-permute-done((bf16[512,1024]{1,0:T(8,128)(2,1)S(1)}, bf16[512,1024]{1,0:T(8,128)(2,1)S(1)}, u32[]{:S(2)}, u32[]{:S(2)}) %collective-permute-start.22) | collective-permute-done | bytes 1048608 | tf_op jit(solution)/shard_map/ppermute | solution.py:345
  112.6 0.5 collective-permute-start.25
  113.3 3.1 %collective-permute-start.26 = (bf16[256,1024]{1,0:T(8,128)(2,1)S(1)}, bf16[256,1024]{1,0:T(8,128)(2,1)S(1)}, u32[]{:S(2)}, u32[]{:S(2)}) collective-permute-start(bf16[256,1024]{1,0:T(8,128)(2,1)S(1)} %add_convert_fusion.4), channel_id=1, source_target_pairs={{0,6},{1,7},{2,0},{3,1},{4,2},{5,3},{6,4},{7,5},{8,14},{9,15},{10,... | collective-permute-start | bytes 1572872 | tf_op jit(solution)/shard_map/ppermute | solution.py:345
  116.3 12.7 %product.4 = (bf16[512,1024]{1,0:T(8,128)(2,1)S(1)}, bf16[512,1024]{1,0:T(8,128)(2,1)S(1)}, f32[256,1024]{1,0:T(8,128)S(1)}, f32[256,1024]{1,0:T(8,128)S(1)}, f32[512,1024]{1,0:T(8,128)S(1)}) custom-call(s32[4]{0:T(128)S(1)} %pad_add_fusion.cols, bf16[512,1024]{1,0:T(8,128)(2,1)S(1)} %attend.1.refs_0_, ...), custom_call_target="tpu_custom_call" | custom-call | flops 34359738368 | bytes 10485760 | tf_op jit(solution)/shard_map/product/pallas_call | solution.py:304
  129.1 3.2 %collective-permute-start.29 = (bf16[512,1024]{1,0:T(8,128)(2,1)S(1)}, bf16[512,1024]{1,0:T(8,128)(2,1)S(1)}, u32[]{:S(2)}, u32[]{:S(2)}) collective-permute-start(bf16[512,1024]{1,0:T(8,128)(2,1)S(1)} %get-tuple-element.42), channel_id=1, source_target_pairs={{0,6},{1,7},{2,0},{3,1},{4,2},{5,3},{6,4},{7,5},{8,14},{9,15},{10,... | collective-permute-start | bytes 3145736 | tf_op jit(solution)/shard_map/ppermute | solution.py:345
  132.3 5.1 %product.5 = f32[512,1024]{1,0:T(8,128)S(1)} custom-call(s32[4]{0:T(128)S(1)} %pad_add_fusion.cols, bf16[512,1024]{1,0:T(8,128)(2,1)S(1)} %attend.1.refs_0_, bf16[512,1024]{1,0:T(8,128)(2,1)S(1)} %collective-permute-done.24.refs_1_, bf16[1024,8192]{1,0:T(8,128)(2,1)} %refs_2_.3, bf16[1024,8192]{1,0:T(8,128)(2,1)} %collective-permute-done.21.refs_3_.refs_5_), custom_call_target="tpu_custom_call" | custom-call | flops 8589934592 | bytes 4194304 | tf_op jit(solution)/shard_map/product/pallas_call | solution.py:304
  137.5 17.0 %collective-permute-done.27 = bf16[512,1024]{1,0:T(8,128)(2,1)S(1)} collective-permute-done((bf16[512,1024]{1,0:T(8,128)(2,1)S(1)}, bf16[512,1024]{1,0:T(8,128)(2,1)S(1)}, u32[]{:S(2)}, u32[]{:S(2)}) %collective-permute-start.27) | collective-permute-done | bytes 1048608 | tf_op jit(solution)/shard_map/ppermute | solution.py:345
  154.9 3.3 %collective-permute-start.30 = (bf16[256,1024]{1,0:T(8,128)(2,1)S(1)}, bf16[256,1024]{1,0:T(8,128)(2,1)S(1)}, u32[]{:S(2)}, u32[]{:S(2)}) collective-permute-start(bf16[256,1024]{1,0:T(8,128)(2,1)S(1)} %add_convert_fusion), channel_id=1, source_target_pairs={{0,6},{1,7},{2,0},{3,1},{4,2},{5,3},{6,4},{7,5},{8,14},{9,15},{10,... | collective-permute-start | bytes 1572872 | tf_op jit(solution)/shard_map/ppermute | solution.py:345
  158.2 0.5 add_convert_fusion.3
  158.7 9.1 %collective-permute-done.28 = bf16[256,1024]{1,0:T(8,128)(2,1)S(1)} collective-permute-done((bf16[256,1024]{1,0:T(8,128)(2,1)S(1)}, bf16[256,1024]{1,0:T(8,128)(2,1)S(1)}, u32[]{:S(2)}, u32[]{:S(2)}) %collective-permute-start.28) | collective-permute-done | bytes 524320 | tf_op jit(solution)/shard_map/ppermute | solution.py:345
  167.9 0.6 fusion.3
  168.4 1.5 pad_maximum_fusion
  (83 shorter events, 4.6 us)
Async XLA Ops:
  0.0 75.3 %collective-permute-start.21 = (bf16[1024,8192]{1,0:T(8,128)(2,1)}, bf16[1024,8192]{1,0:T(8,128)(2,1)}, u32[]{:S(2)}, u32[]{:S(2)}) collective-permute-start(bf16[1024,8192]{1,0:T(8,128)(2,1)} %refs_2_.3), channel_id=1, source_target_pairs={{0,1},{1,0},{2,3},{3,2},{4,5},{5,4},{6,7},{7,6},{8,9},{9,8},{10,11... | collective-permute-start | bytes 50331656 | tf_op jit(solution)/shard_map/ppermute | solution.py:342
  0.0 10.2 %collective-permute-start = (bf16[1024,128]{1,0:T(8,128)(2,1)}, bf16[1024,128]{1,0:T(8,128)(2,1)S(1)}, u32[]{:S(2)}, u32[]{:S(2)}) collective-permute-start(bf16[1024,128]{1,0:T(8,128)(2,1)} %param.8), channel_id=1, source_target_pairs={{0,8},{8,16},{16,24},{24,0},{32,40},{40,48},{48,56},{56,32},{64,72... | collective-permute-start | bytes 786440 | tf_op jit(solution)/shard_map/ppermute | solution.py:41
  1.5 9.1 %collective-permute-start.1 = (bf16[1024,128]{1,0:T(8,128)(2,1)}, bf16[1024,128]{1,0:T(8,128)(2,1)S(1)}, u32[]{:S(2)}, u32[]{:S(2)}) collective-permute-start(bf16[1024,128]{1,0:T(8,128)(2,1)} %param.8), channel_id=1, source_target_pairs={{0,24},{8,0},{16,8},{24,16},{32,56},{40,32},{48,40},{56,48},{64,88... | collective-permute-start | bytes 786440 | tf_op jit(solution)/shard_map/ppermute | solution.py:42
  3.2 10.4 %collective-permute-start.10 = (bf16[1024,128]{1,0:T(8,128)(2,1)}, bf16[1024,128]{1,0:T(8,128)(2,1)S(1)}, u32[]{:S(2)}, u32[]{:S(2)}) collective-permute-start(bf16[1024,128]{1,0:T(8,128)(2,1)} %param.9), channel_id=1, source_target_pairs={{0,32},{8,40},{16,48},{24,56},{32,64},{40,72},{48,80},{56,88},{64,... | collective-permute-start | bytes 786440 | tf_op jit(solution)/shard_map/ppermute | solution.py:41
  3.2 11.7 %collective-permute-start.11 = (bf16[1024,128]{1,0:T(8,128)(2,1)}, bf16[1024,128]{1,0:T(8,128)(2,1)S(1)}, u32[]{:S(2)}, u32[]{:S(2)}) collective-permute-start(bf16[1024,128]{1,0:T(8,128)(2,1)} %param.9), channel_id=1, source_target_pairs={{0,96},{8,104},{16,112},{24,120},{32,0},{40,8},{48,16},{56,24},{64... | collective-permute-start | bytes 786440 | tf_op jit(solution)/shard_map/ppermute | solution.py:42
  10.3 6.4 %collective-permute-start.2 = (bf16[512,128]{1,0:T(8,128)(2,1)S(1)}, bf16[512,128]{1,0:T(8,128)(2,1)S(1)}, u32[]{:S(2)}, u32[]{:S(2)}) collective-permute-start(bf16[512,128]{1,0:T(8,128)(2,1)S(1)} %slice.132), channel_id=1, source_target_pairs={{0,8},{8,16},{16,24},{24,0},{32,40},{40,48},{48,56},{56,32},{64,72... | collective-permute-start | bytes 393224 | tf_op jit(solution)/shard_map/ppermute | solution.py:43
  10.6 6.5 %collective-permute-start.3 = (bf16[512,128]{1,0:T(8,128)(2,1)S(1)}, bf16[512,128]{1,0:T(8,128)(2,1)S(1)}, u32[]{:S(2)}, u32[]{:S(2)}) collective-permute-start(bf16[512,128]{1,0:T(8,128)(2,1)S(1)} %slice.133), channel_id=1, source_target_pairs={{0,24},{8,0},{16,8},{24,16},{32,56},{40,32},{48,40},{56,48},{64,88... | collective-permute-start | bytes 393224 | tf_op jit(solution)/shard_map/ppermute | solution.py:44
  13.7 5.1 %collective-permute-start.12 = (bf16[512,128]{1,0:T(8,128)(2,1)S(1)}, bf16[512,128]{1,0:T(8,128)(2,1)S(1)}, u32[]{:S(2)}, u32[]{:S(2)}) collective-permute-start(bf16[512,128]{1,0:T(8,128)(2,1)S(1)} %slice.134), channel_id=1, source_target_pairs={{0,32},{8,40},{16,48},{24,56},{32,64},{40,72},{48,80},{56,88},{64,... | collective-permute-start | bytes 393224 | tf_op jit(solution)/shard_map/ppermute | solution.py:43
  15.0 32.9 %copy-start.2 = (bf16[1024,1024]{1,0:T(8,128)(2,1)S(1)}, bf16[1024,1024]{1,0:T(8,128)(2,1)}, u32[]{:S(2)}) copy-start(bf16[1024,1024]{1,0:T(8,128)(2,1)} %param.7) | copy-start | bytes 6291460
  15.0 7.0 %collective-permute-start.13 = (bf16[512,128]{1,0:T(8,128)(2,1)S(1)}, bf16[512,128]{1,0:T(8,128)(2,1)S(1)}, u32[]{:S(2)}, u32[]{:S(2)}) collective-permute-start(bf16[512,128]{1,0:T(8,128)(2,1)S(1)} %slice.135), channel_id=1, source_target_pairs={{0,96},{8,104},{16,112},{24,120},{32,0},{40,8},{48,16},{56,24},{64... | collective-permute-start | bytes 393224 | tf_op jit(solution)/shard_map/ppermute | solution.py:44
  16.6 14.5 %copy-start.4 = (bf16[2048,128]{1,0:T(8,128)(2,1)}, bf16[2048,128]{1,0:T(8,128)(2,1)S(1)}, u32[]{:S(2)}) copy-start(bf16[2048,128]{1,0:T(8,128)(2,1)S(1)} %constant_dynamic-update-slice_fusion.refs_0_) | copy-start | bytes 1572868
  16.7 5.4 %copy-start.3 = (bf16[2048,128]{1,0:T(8,128)(2,1)}, bf16[2048,128]{1,0:T(8,128)(2,1)S(1)}, u32[]{:S(2)}) copy-start(bf16[2048,128]{1,0:T(8,128)(2,1)S(1)} %constant_dynamic-update-slice_fusion.5.refs_8_) | copy-start | bytes 1572868
  16.7 12.4 %collective-permute-start.16 = (bf16[2048,128]{1,0:T(8,128)(2,1)S(1)}, bf16[2048,128]{1,0:T(8,128)(2,1)S(1)}, u32[]{:S(2)}, u32[]{:S(2)}) collective-permute-start(bf16[2048,128]{1,0:T(8,128)(2,1)S(1)} %constant_dynamic-update-slice_fusion.5.refs_8_), channel_id=1, source_target_pairs={{0,24},{8,0},{16,8},{24,16},{32,56},{40,32},{48,40},{56,48},{64,88... | collective-permute-start | bytes 1572872 | tf_op jit(solution)/shard_map/ppermute | solution.py:54
  17.1 14.0 %collective-permute-start.14 = (bf16[2048,128]{1,0:T(8,128)(2,1)S(1)}, bf16[2048,128]{1,0:T(8,128)(2,1)}, u32[]{:S(2)}, u32[]{:S(2)}) collective-permute-start(bf16[2048,128]{1,0:T(8,128)(2,1)S(1)} %constant_dynamic-update-slice_fusion.5.refs_8_), channel_id=1, source_target_pairs={{0,8},{8,16},{16,24},{24,0},{32,40},{40,48},{48,56},{56,32},{64,72... | collective-permute-start | bytes 1572872 | tf_op jit(solution)/shard_map/ppermute | solution.py:54
  18.8 13.7 %collective-permute-start.6 = (bf16[2048,128]{1,0:T(8,128)(2,1)S(1)}, bf16[2048,128]{1,0:T(8,128)(2,1)S(1)}, u32[]{:S(2)}, u32[]{:S(2)}) collective-permute-start(bf16[2048,128]{1,0:T(8,128)(2,1)S(1)} %constant_dynamic-update-slice_fusion.refs_0_), channel_id=1, source_target_pairs={{0,96},{8,104},{16,112},{24,120},{32,0},{40,8},{48,16},{56,24},{64... | collective-permute-start | bytes 1572872 | tf_op jit(solution)/shard_map/ppermute | solution.py:54
  22.0 10.9 %collective-permute-start.4 = (bf16[2048,128]{1,0:T(8,128)(2,1)S(1)}, bf16[2048,128]{1,0:T(8,128)(2,1)}, u32[]{:S(2)}, u32[]{:S(2)}) collective-permute-start(bf16[2048,128]{1,0:T(8,128)(2,1)S(1)} %constant_dynamic-update-slice_fusion.refs_0_), channel_id=1, source_target_pairs={{0,32},{8,40},{16,48},{24,56},{32,64},{40,72},{48,80},{56,88},{64,... | collective-permute-start | bytes 1572872 | tf_op jit(solution)/shard_map/ppermute | solution.py:54
  23.4 24.4 %copy-start.5 = (bf16[2048,128]{1,0:T(8,128)(2,1)}, bf16[2048,128]{1,0:T(8,128)(2,1)S(1)}, u32[]{:S(2)}) copy-start(bf16[2048,128]{1,0:T(8,128)(2,1)S(1)} %constant_dynamic-update-slice_fusion.7.refs_9_) | copy-start | bytes 1572868
  29.1 6.7 %copy-start.6 = (bf16[2048,128]{1,0:T(8,128)(2,1)}, bf16[2048,128]{1,0:T(8,128)(2,1)S(1)}, u32[]{:S(2)}) copy-start(bf16[2048,128]{1,0:T(8,128)(2,1)S(1)} %collective-permute-done.16.refs_12_) | copy-start | bytes 1572868
  29.1 11.6 %collective-permute-start.17 = (bf16[2048,128]{1,0:T(8,128)(2,1)S(1)}, bf16[2048,128]{1,0:T(8,128)(2,1)}, u32[]{:S(2)}, u32[]{:S(2)}) collective-permute-start(bf16[2048,128]{1,0:T(8,128)(2,1)S(1)} %constant_dynamic-update-slice_fusion.7.refs_9_), channel_id=1, source_target_pairs={{0,24},{8,0},{16,8},{24,16},{32,56},{40,32},{48,40},{56,48},{64,88... | collective-permute-start | bytes 1572872 | tf_op jit(solution)/shard_map/ppermute | solution.py:54
  31.1 14.3 %collective-permute-start.15 = (bf16[2048,128]{1,0:T(8,128)(2,1)S(1)}, bf16[2048,128]{1,0:T(8,128)(2,1)}, u32[]{:S(2)}, u32[]{:S(2)}) collective-permute-start(bf16[2048,128]{1,0:T(8,128)(2,1)S(1)} %constant_dynamic-update-slice_fusion.7.refs_9_), channel_id=1, source_target_pairs={{0,8},{8,16},{16,24},{24,0},{32,40},{40,48},{48,56},{56,32},{64,72... | collective-permute-start | bytes 1572872 | tf_op jit(solution)/shard_map/ppermute | solution.py:54
  32.5 3.3 %copy-start.7 = (bf16[2048,128]{1,0:T(8,128)(2,1)}, bf16[2048,128]{1,0:T(8,128)(2,1)S(1)}, u32[]{:S(2)}) copy-start(bf16[2048,128]{1,0:T(8,128)(2,1)S(1)} %collective-permute-done.6.refs_4_) | copy-start | bytes 1572868
  32.5 14.7 %collective-permute-start.7 = (bf16[2048,128]{1,0:T(8,128)(2,1)}, bf16[2048,128]{1,0:T(8,128)(2,1)}, u32[]{:S(2)}, u32[]{:S(2)}) collective-permute-start(bf16[2048,128]{1,0:T(8,128)(2,1)} %constant_dynamic-update-slice_fusion.2.refs_1_), channel_id=1, source_target_pairs={{0,96},{8,104},{16,112},{24,120},{32,0},{40,8},{48,16},{56,24},{64... | collective-permute-start | bytes 1572872 | tf_op jit(solution)/shard_map/ppermute | solution.py:54
  32.8 14.4 %collective-permute-start.5 = (bf16[2048,128]{1,0:T(8,128)(2,1)}, bf16[2048,128]{1,0:T(8,128)(2,1)}, u32[]{:S(2)}, u32[]{:S(2)}) collective-permute-start(bf16[2048,128]{1,0:T(8,128)(2,1)} %constant_dynamic-update-slice_fusion.2.refs_1_), channel_id=1, source_target_pairs={{0,32},{8,40},{16,48},{24,56},{32,64},{40,72},{48,80},{56,88},{64,... | collective-permute-start | bytes 1572872 | tf_op jit(solution)/shard_map/ppermute | solution.py:54
  40.7 14.5 %collective-permute-start.18 = (bf16[2048,128]{1,0:T(8,128)(2,1)}, bf16[2048,128]{1,0:T(8,128)(2,1)}, u32[]{:S(2)}, u32[]{:S(2)}) collective-permute-start(bf16[2048,128]{1,0:T(8,128)(2,1)} %collective-permute-done.14.refs_10_), channel_id=1, source_target_pairs={{0,8},{8,16},{16,24},{24,0},{32,40},{40,48},{48,56},{56,32},{64,72... | collective-permute-start | bytes 1572872 | tf_op jit(solution)/shard_map/ppermute | solution.py:54
  45.4 10.8 %collective-permute-start.8 = (bf16[2048,128]{1,0:T(8,128)(2,1)}, bf16[2048,128]{1,0:T(8,128)(2,1)}, u32[]{:S(2)}, u32[]{:S(2)}) collective-permute-start(bf16[2048,128]{1,0:T(8,128)(2,1)} %collective-permute-done.4.refs_2_), channel_id=1, source_target_pairs={{0,32},{8,40},{16,48},{24,56},{32,64},{40,72},{48,80},{56,88},{64,... | collective-permute-start | bytes 1572872 | tf_op jit(solution)/shard_map/ppermute | solution.py:54
  47.2 9.5 %collective-permute-start.19 = (bf16[2048,128]{1,0:T(8,128)(2,1)}, bf16[2048,128]{1,0:T(8,128)(2,1)}, u32[]{:S(2)}, u32[]{:S(2)}) collective-permute-start(bf16[2048,128]{1,0:T(8,128)(2,1)} %collective-permute-done.17.refs_13_), channel_id=1, source_target_pairs={{0,24},{8,0},{16,8},{24,16},{32,56},{40,32},{48,40},{56,48},{64,88... | collective-permute-start | bytes 1572872 | tf_op jit(solution)/shard_map/ppermute | solution.py:54
  47.2 11.5 %collective-permute-start.9 = (bf16[2048,128]{1,0:T(8,128)(2,1)}, bf16[2048,128]{1,0:T(8,128)(2,1)}, u32[]{:S(2)}, u32[]{:S(2)}) collective-permute-start(bf16[2048,128]{1,0:T(8,128)(2,1)} %collective-permute-done.7.refs_5_), channel_id=1, source_target_pairs={{0,96},{8,104},{16,112},{24,120},{32,0},{40,8},{48,16},{56,24},{64... | collective-permute-start | bytes 1572872 | tf_op jit(solution)/shard_map/ppermute | solution.py:54
  72.6 2.7 %collective-permute-start.20 = (bf16[512,1024]{1,0:T(8,128)(2,1)S(1)}, bf16[512,1024]{1,0:T(8,128)(2,1)S(1)}, u32[]{:S(2)}, u32[]{:S(2)}) collective-permute-start(bf16[512,1024]{1,0:T(8,128)(2,1)S(1)} %get-tuple-element.28.refs_0_.refs_2_), channel_id=1, source_target_pairs={{0,1},{1,0},{2,3},{3,2},{4,5},{5,4},{6,7},{7,6},{8,9},{9,8},{10,11... | collective-permute-start | bytes 3145736 | tf_op jit(solution)/shard_map/ppermute | solution.py:369
  72.8 16.2 %copy-start = (bf16[16384,128]{1,0:T(8,128)(2,1)S(1)}, bf16[16384,128]{1,0:T(8,128)(2,1)}, u32[]{:S(2)}) copy-start(bf16[16384,128]{1,0:T(8,128)(2,1)} %get-tuple-element.31.k_all) | copy-start | bytes 12582916
  72.8 16.2 %copy-start.1 = (bf16[16384,128]{1,0:T(8,128)(2,1)S(1)}, bf16[16384,128]{1,0:T(8,128)(2,1)}, u32[]{:S(2)}) copy-start(bf16[16384,128]{1,0:T(8,128)(2,1)} %get-tuple-element.32.v_all) | copy-start | bytes 12582916
  85.6 26.8 %collective-permute-start.22 = (bf16[512,1024]{1,0:T(8,128)(2,1)S(1)}, bf16[512,1024]{1,0:T(8,128)(2,1)S(1)}, u32[]{:S(2)}, u32[]{:S(2)}) collective-permute-start(bf16[512,1024]{1,0:T(8,128)(2,1)S(1)} %get-tuple-element.33), channel_id=1, source_target_pairs={{0,2},{1,3},{2,4},{3,5},{4,6},{5,7},{6,0},{7,1},{8,10},{9,11},{10,... | collective-permute-start | bytes 3145736 | tf_op jit(solution)/shard_map/ppermute | solution.py:345
  87.4 25.7 %collective-permute-start.23 = (bf16[512,1024]{1,0:T(8,128)(2,1)S(1)}, bf16[512,1024]{1,0:T(8,128)(2,1)S(1)}, u32[]{:S(2)}, u32[]{:S(2)}) collective-permute-start(bf16[512,1024]{1,0:T(8,128)(2,1)S(1)} %get-tuple-element.35), channel_id=1, source_target_pairs={{0,6},{1,7},{2,0},{3,1},{4,2},{5,3},{6,4},{7,5},{8,14},{9,15},{10,... | collective-permute-start | bytes 3145736 | tf_op jit(solution)/shard_map/ppermute | solution.py:345
  99.2 17.1 %collective-permute-start.24 = (bf16[512,1024]{1,0:T(8,128)(2,1)S(1)}, bf16[512,1024]{1,0:T(8,128)(2,1)S(1)}, u32[]{:S(2)}, u32[]{:S(2)}) collective-permute-start(bf16[512,1024]{1,0:T(8,128)(2,1)S(1)} %attend.1.refs_0_), channel_id=1, source_target_pairs={{0,1},{1,0},{2,3},{3,2},{4,5},{5,4},{6,7},{7,6},{8,9},{9,8},{10,11... | collective-permute-start | bytes 3145736 | tf_op jit(solution)/shard_map/ppermute | solution.py:369
  112.6 19.8 %collective-permute-start.25 = (bf16[256,1024]{1,0:T(8,128)(2,1)S(1)}, bf16[256,1024]{1,0:T(8,128)(2,1)S(1)}, u32[]{:S(2)}, u32[]{:S(2)}) collective-permute-start(bf16[256,1024]{1,0:T(8,128)(2,1)S(1)} %add_convert_fusion.5), channel_id=1, source_target_pairs={{0,2},{1,3},{2,4},{3,5},{4,6},{5,7},{6,0},{7,1},{8,10},{9,11},{10,... | collective-permute-start | bytes 1572872 | tf_op jit(solution)/shard_map/ppermute | solution.py:345
  113.3 19.1 %collective-permute-start.26 = (bf16[256,1024]{1,0:T(8,128)(2,1)S(1)}, bf16[256,1024]{1,0:T(8,128)(2,1)S(1)}, u32[]{:S(2)}, u32[]{:S(2)}) collective-permute-start(bf16[256,1024]{1,0:T(8,128)(2,1)S(1)} %add_convert_fusion.4), channel_id=1, source_target_pairs={{0,6},{1,7},{2,0},{3,1},{4,2},{5,3},{6,4},{7,5},{8,14},{9,15},{10,... | collective-permute-start | bytes 1572872 | tf_op jit(solution)/shard_map/ppermute | solution.py:345
  129.0 25.4 %collective-permute-start.27 = (bf16[512,1024]{1,0:T(8,128)(2,1)S(1)}, bf16[512,1024]{1,0:T(8,128)(2,1)S(1)}, u32[]{:S(2)}, u32[]{:S(2)}) collective-permute-start(bf16[512,1024]{1,0:T(8,128)(2,1)S(1)} %get-tuple-element.41), channel_id=1, source_target_pairs={{0,2},{1,3},{2,4},{3,5},{4,6},{5,7},{6,0},{7,1},{8,10},{9,11},{10,... | collective-permute-start | bytes 3145736 | tf_op jit(solution)/shard_map/ppermute | solution.py:345
  129.1 25.6 %collective-permute-start.29 = (bf16[512,1024]{1,0:T(8,128)(2,1)S(1)}, bf16[512,1024]{1,0:T(8,128)(2,1)S(1)}, u32[]{:S(2)}, u32[]{:S(2)}) collective-permute-start(bf16[512,1024]{1,0:T(8,128)(2,1)S(1)} %get-tuple-element.42), channel_id=1, source_target_pairs={{0,6},{1,7},{2,0},{3,1},{4,2},{5,3},{6,4},{7,5},{8,14},{9,15},{10,... | collective-permute-start | bytes 3145736 | tf_op jit(solution)/shard_map/ppermute | solution.py:345
  154.6 13.2 %collective-permute-start.28 = (bf16[256,1024]{1,0:T(8,128)(2,1)S(1)}, bf16[256,1024]{1,0:T(8,128)(2,1)S(1)}, u32[]{:S(2)}, u32[]{:S(2)}) collective-permute-start(bf16[256,1024]{1,0:T(8,128)(2,1)S(1)} %add_convert_fusion.1), channel_id=1, source_target_pairs={{0,2},{1,3},{2,4},{3,5},{4,6},{5,7},{6,0},{7,1},{8,10},{9,11},{10,... | collective-permute-start | bytes 1572872 | tf_op jit(solution)/shard_map/ppermute | solution.py:345
  154.9 13.0 %collective-permute-start.30 = (bf16[256,1024]{1,0:T(8,128)(2,1)S(1)}, bf16[256,1024]{1,0:T(8,128)(2,1)S(1)}, u32[]{:S(2)}, u32[]{:S(2)}) collective-permute-start(bf16[256,1024]{1,0:T(8,128)(2,1)S(1)} %add_convert_fusion), channel_id=1, source_target_pairs={{0,6},{1,7},{2,0},{3,1},{4,2},{5,3},{6,4},{7,5},{8,14},{9,15},{10,... | collective-permute-start | bytes 1572872 | tf_op jit(solution)/shard_map/ppermute | solution.py:345
